TPU v7x, 32 devices: a whole 2x2x4 slice. The times are simulated.
32 devices in a mesh: event: 4 (over z), terrain: 8 (over y, x, core).
Axes of the slice: x: 2, y: 2, z: 4, core: 2. Of those that a mesh axis runs over, the one named last changes fastest.
Arguments:
- level_start: float32 [4, 256, 1024], P('event', 'terrain'), may hold values from -18 to 18
- bed_depth: float32 [256, 1024], P('terrain'), may hold values from 0.5 to 2
- wet_bits: int32 [4, 256, 1024], P('event', 'terrain'), may hold values from 0 to 255
- tile_owner: int32 [2048, 1], P('terrain'), may hold values from 0 to 7; in each aligned block of 256 rows (0 to 255, 256 to 511, ...) at most 48 rows name the same one
- vuln_weight: bfloat16 [128, 256], replicated, may hold values from -0.5 to 0.5
- vuln_bias: float32 [256], replicated, may hold values from -2 to 2
- account_index: int32 [3072, 128], P('terrain'), may hold values from 0 to 1023
- bin_index: int32 [3072, 128], P('terrain'), may hold values from 0 to 255
- exposure_value: bfloat16 [3072, 128], P('terrain'), may hold values from 1 to 10
- deductible: float32 [1024], replicated, may hold values from 0 to 0.8
- limit: float32 [1024], replicated, may hold values from 0.5 to 1.5
Outputs:
- level: float32 [4, 256, 1024], P('event', 'terrain')
- net_loss: bfloat16 [4, 1024, 256], P('event')
- portfolio: float32 [1024, 256], P('terrain')
Inputs may be any that keep to these rules, and one draw needn't show every extreme that they name: `tile_owner`: among the 256 tiles of one device no owner is named more than 48 times; in some devices one owner is named exactly 48 times. `wet_bits`: bit s (the value // 2**s, mod 2) is 1 where the cell is wet in substep s. `account_index`: rows of an owner's records that no tile reaches are not read.
All inputs are finite; a program needn't handle non-finite values.
Results may differ from a plain program's by a relative error of at most 0.0004.
The roundings to bfloat16 on the way count: a program that leaves them out, or rounds other values in their place, can miss the bound.
Values may be sent and summed in bfloat16 or wider, within the bound.
A program may use at most 64 MiB of HBM per device.

v0:
```python
import functools

import jax
import jax.numpy as jnp
from jax import lax
from jax.experimental import pallas as pl
from jax.experimental.pallas import tpu as pltpu
from jax.sharding import PartitionSpec as P

SUBSTEPS = 8
CHUNK = 8
HALVES = 2
LOW = 256

courant = 0.5
gravity = 1.0

VMEM = pl.BlockSpec(memory_space=pltpu.VMEM)
SMEM = pl.BlockSpec(memory_space=pltpu.SMEM)
MESH = pl.DeviceIdType.MESH


def exchange_kernel(jobs, *refs):
    count = len(jobs)
    sources, targets, sems = refs[:count], refs[count : 2 * count], refs[2 * count :]
    barrier = pltpu.get_barrier_semaphore()
    greeted = 0
    for axis in dict.fromkeys(axis for axis, _ in jobs):
        size = lax.axis_size(axis)
        me = lax.axis_index(axis)
        for hop in range(1, size):
            pl.semaphore_signal(
                barrier, inc=1, device_id={axis: lax.rem(me + hop, size)}, device_id_type=MESH
            )
        greeted += size - 1
    pl.semaphore_wait(barrier, greeted)
    copies = []
    for job, (axis, spread) in enumerate(jobs):
        source, target = sources[job], targets[job]
        local, sent, received = sems[3 * job : 3 * job + 3]
        size = lax.axis_size(axis)
        me = lax.axis_index(axis)
        for hop in range(1, size):
            peer = lax.rem(me + hop, size)
            copy = pltpu.make_async_remote_copy(
                src_ref=source if spread else source.at[peer],
                dst_ref=target.at[me],
                send_sem=sent.at[hop],
                recv_sem=received.at[hop],
                device_id={axis: peer},
                device_id_type=MESH,
            )
            copy.start()
            copies.append(copy)
        own = pltpu.make_async_copy(source if spread else source.at[me], target.at[me], local)
        own.start()
        copies.append(own)
    for copy in copies:
        copy.wait()


def exchange(arrays, jobs, number):
    shapes, scratch = [], []
    for array, (axis, spread) in zip(arrays, jobs):
        size = lax.axis_size(axis)
        shape = (size,) + array.shape if spread else array.shape
        shapes.append(jax.ShapeDtypeStruct(shape, array.dtype))
        scratch += [
            pltpu.SemaphoreType.DMA,
            pltpu.SemaphoreType.DMA((size,)),
            pltpu.SemaphoreType.DMA((size,)),
        ]
    return pl.pallas_call(
        functools.partial(exchange_kernel, jobs),
        out_shape=shapes,
        in_specs=[VMEM] * len(arrays),
        out_specs=[VMEM] * len(arrays),
        scratch_shapes=scratch,
        compiler_params=pltpu.CompilerParams(collective_id=number, has_side_effects=True),
        name="exchange" + str(number),
    )(*arrays)


def halo_kernel(*refs):
    count = (len(refs) - 2) // 3
    fields, above, below = refs[:count], refs[count : 2 * count], refs[2 * count : 3 * count]
    sent, received = refs[3 * count :]
    size = lax.axis_size("terrain")
    me = lax.axis_index("terrain")
    later, earlier = lax.rem(me + 1, size), lax.rem(me + size - 1, size)
    barrier = pltpu.get_barrier_semaphore()
    for peer in (later, earlier):
        pl.semaphore_signal(barrier, inc=1, device_id={"terrain": peer}, device_id_type=MESH)
    pl.semaphore_wait(barrier, 2)
    copies = []
    for side, (peer, targets) in enumerate(((later, above), (earlier, below))):
        for i in range(count):
            first = 0 if side else fields[i].shape[0] - SUBSTEPS
            copy = pltpu.make_async_remote_copy(
                src_ref=fields[i].at[pl.ds(first, SUBSTEPS)],
                dst_ref=targets[i],
                send_sem=sent.at[side * count + i],
                recv_sem=received.at[side * count + i],
                device_id={"terrain": peer},
                device_id_type=MESH,
            )
            copy.start()
            copies.append(copy)
    for copy in copies:
        copy.wait()


def halos(fields, number):
    shapes = [jax.ShapeDtypeStruct((SUBSTEPS,) + f.shape[1:], f.dtype) for f in fields] * 2
    return pl.pallas_call(
        halo_kernel,
        out_shape=shapes,
        in_specs=[VMEM] * len(fields),
        out_specs=[VMEM] * len(shapes),
        scratch_shapes=[pltpu.SemaphoreType.DMA((len(shapes),))] * 2,
        compiler_params=pltpu.CompilerParams(collective_id=number, has_side_effects=True),
        name="halos",
    )(*fields)


def settle_kernel(
    scale, parts, floor, roof, net_loss, portfolio,
    made, made_low, kept, kept_low, arrived, summed, kept_sum, local,
    sent_low, got_low, sent_net, got_net, sent_sum, got_sum,
):
    owners, share_rows, _ = parts.shape
    events = lax.axis_size("event")
    me, group = lax.axis_index("terrain"), lax.axis_index("event")
    barrier = pltpu.get_barrier_semaphore()
    for axis, size, mine in (("terrain", owners, me), ("event", events, group)):
        for hop in range(1, size):
            pl.semaphore_signal(
                barrier, inc=1, device_id={axis: lax.rem(mine + hop, size)}, device_id_type=MESH
            )
    whole = parts[0]
    for n in range(1, owners):
        whole = whole + parts[n]
    picked = (share_rows, floor.shape[1])
    account = lax.broadcasted_iota(jnp.int32, picked, 1)
    mine = account == lax.broadcasted_iota(jnp.int32, picked, 0) + me * share_rows

    def of_share(terms):
        return jnp.sum(jnp.where(mine, terms[...], 0.0), axis=1, keepdims=True)

    net = jnp.minimum(jnp.maximum(whole * scale - of_share(floor), 0.0), of_share(roof))
    made[...] = net.reshape(made.shape)
    made_low[...] = net.astype(made_low.dtype)
    first = [
        pltpu.make_async_copy(made, kept, local.at[0]),
        pltpu.make_async_copy(made_low, kept_low, local.at[1]),
    ]
    for copy in first:
        copy.start()
    pl.semaphore_wait(barrier, owners + events - 2)
    for copy in first:
        copy.wait()

    def push(axis, size, index, source, target, sent, received, split):
        copies = []
        for hop in range(1, size):
            peer = lax.rem(index + hop, size)
            copy = pltpu.make_async_remote_copy(
                src_ref=source.at[peer] if split else source,
                dst_ref=target.at[index],
                send_sem=sent.at[hop],
                recv_sem=received.at[hop],
                device_id={axis: peer},
                device_id_type=MESH,
            )
            copy.start()
            copies.append(copy)
        return copies

    nets = push("event", events, group, kept, arrived, sent_net, got_net, True)
    own_net = pltpu.make_async_copy(kept.at[group], arrived.at[group], local.at[2])
    own_net.start()
    lows = push("terrain", owners, me, kept_low, net_loss, sent_low, got_low, False)
    own_low = pltpu.make_async_copy(kept_low, net_loss.at[me], local.at[3])
    own_low.start()
    for copy in nets + [own_net]:
        copy.wait()
    total = arrived[0]
    for n in range(1, events):
        total = total + arrived[n]
    summed[...] = total / events
    last = pltpu.make_async_copy(summed, kept_sum, local.at[4])
    last.start()
    last.wait()
    sums = push("event", events, group, kept_sum, portfolio, sent_sum, got_sum, False)
    own_sum = pltpu.make_async_copy(kept_sum, portfolio.at[group], local.at[5])
    own_sum.start()
    for copy in sums + [own_sum] + lows + [own_low]:
        copy.wait()


def settle(parts, floor, roof, scale, number):
    owners, share_rows, bins = parts.shape
    events = lax.axis_size("event")
    split = (events, share_rows // events, bins)
    dma = pltpu.SemaphoreType.DMA
    return pl.pallas_call(
        functools.partial(settle_kernel, scale),
        out_shape=(
            jax.ShapeDtypeStruct((owners, share_rows, bins), jnp.bfloat16),
            jax.ShapeDtypeStruct(split, jnp.float32),
        ),
        in_specs=[VMEM] * 3,
        out_specs=(VMEM, VMEM),
        scratch_shapes=[
            pltpu.VMEM(split, jnp.float32),
            pltpu.VMEM((share_rows, bins), jnp.bfloat16),
            pltpu.VMEM(split, jnp.float32),
            pltpu.VMEM((share_rows, bins), jnp.bfloat16),
            pltpu.VMEM(split, jnp.float32),
            pltpu.VMEM(split[1:], jnp.float32),
            pltpu.VMEM(split[1:], jnp.float32),
            dma((6,)),
        ]
        + [dma((owners,))] * 2
        + [dma((events,))] * 4,
        compiler_params=pltpu.CompilerParams(collective_id=number, has_side_effects=True),
        name="settle",
    )(parts, floor, roof)


def flood_kernel(
    rows, slot_count, capacity, level_here, bed_here, wet_here,
    level_above, bed_above, wet_above, level_below, bed_below, wet_below,
    owner_row, weight, bias, level_out, outgoing_out,
):
    first_row = lax.axis_index("terrain") * rows - SUBSTEPS
    total_rows = rows * lax.axis_size("terrain")
    level = jnp.concatenate([level_above[...], level_here[...], level_below[...]], axis=0)
    bed = jnp.concatenate([bed_above[...], bed_here[...], bed_below[...]], axis=0)
    wet = jnp.concatenate([wet_above[...], wet_here[...], wet_below[...]], axis=0)
    shape = level.shape
    tall, width = shape
    row_id = first_row + lax.broadcasted_iota(jnp.int32, shape, 0)
    column = lax.broadcasted_iota(jnp.int32, shape, 1)
    inside = ((row_id >= 0) & (row_id < total_rows)).astype(jnp.float32)
    not_first = (column > 0).astype(jnp.float32)
    not_last = (column < width - 1).astype(jnp.float32)

    def down(field):
        return pltpu.roll(field, tall - 1, 0)

    def up(field):
        return pltpu.roll(field, 1, 0)

    def right(field):
        return pltpu.roll(field, width - 1, 1) * not_last

    def left(field):
        return pltpu.roll(field, 1, 1) * not_first

    level = level * inside
    row_speed = jnp.zeros(shape, jnp.float32)
    col_speed = jnp.zeros(shape, jnp.float32)
    for step in range(SUBSTEPS):
        wet_factor = ((wet >> step) & 1).astype(jnp.float32) * inside
        ld, lu, lr, ll = down(level), up(level), right(level), left(level)
        new_level = 0.25 * (ld + lu + lr + ll)
        if step:
            row_flow, col_flow = bed * row_speed, bed * col_speed
            new_level = new_level - 0.5 * courant * (
                down(row_flow) - up(row_flow) + (right(col_flow) - left(col_flow))
            )
            row_mean = 0.25 * (
                down(row_speed) + up(row_speed) + right(row_speed) + left(row_speed)
            )
            col_mean = 0.25 * (
                down(col_speed) + up(col_speed) + right(col_speed) + left(col_speed)
            )
            row_speed = (row_mean - 0.5 * courant * gravity * (ld - lu)) * wet_factor
            col_speed = (col_mean - 0.5 * courant * gravity * (lr - ll)) * wet_factor
        else:
            row_speed = (0.0 - 0.5 * courant * gravity * (ld - lu)) * wet_factor
            col_speed = (0.0 - 0.5 * courant * gravity * (lr - ll)) * wet_factor
        level = new_level * inside
    level = level[SUBSTEPS : SUBSTEPS + rows]
    level_out[...] = level
    tile = weight.shape[0]
    blocks = width // tile
    pieces = jnp.concatenate(
        [level[:, j * tile : (j + 1) * tile] for j in range(blocks)], axis=0
    ).astype(jnp.bfloat16)
    ratio = jax.nn.sigmoid(
        jnp.dot(pieces, weight[...], preferred_element_type=jnp.float32) + bias[...]
    ).astype(jnp.bfloat16)
    tiles = rows * blocks
    along = lax.broadcasted_iota(jnp.int32, (tiles, tiles), 1)
    across = lax.broadcasted_iota(jnp.int32, (tiles, tiles), 0)

    def number(place):
        return (place % rows) * blocks + place // rows

    owner = jnp.broadcast_to(owner_row[...], (8, tiles)).astype(jnp.float32)
    owner_column = jnp.transpose(owner)[:, :1]
    earlier = (owner_column == owner[:1]) & (number(across) < number(along))
    rank = jnp.sum(earlier.astype(jnp.float32), axis=0, keepdims=True).astype(jnp.int32)
    place = owner_row[...] * capacity + rank
    slot = lax.broadcasted_iota(jnp.int32, (slot_count, tiles), 0)
    chosen = jnp.where(slot == place, 1.0, 0.0).astype(jnp.bfloat16)
    outgoing_out[...] = jnp.dot(chosen, ratio, preferred_element_type=jnp.float32).astype(
        jnp.bfloat16
    )


def loss_kernel(busy, ratio_in, account, threshold, value_in, total, ratio, value, *scratch):
    accounts, bins = total.shape
    slots, tile = account.shape
    high_count = accounts // LOW
    ratio[...] = ratio_in[...].astype(jnp.float32)
    value[...] = value_in[...].astype(jnp.float32)
    halves = len(scratch) // 2
    half = CHUNK // halves
    total[...] = jnp.zeros(total.shape, jnp.float32)
    sub = 16
    low_id = (
        lax.broadcasted_iota(jnp.int32, (LOW, tile), 0).astype(jnp.float32).astype(jnp.bfloat16)
    )
    bin_id = (
        lax.broadcasted_iota(jnp.int32, (sub, bins), 1).astype(jnp.float32).astype(jnp.bfloat16)
    )
    bin_id = jnp.concatenate([bin_id] * (tile // sub), axis=0)

    def rowed(row, height):
        packed = jnp.broadcast_to(row, (sub, row.shape[1])).astype(jnp.bfloat16)
        return jnp.concatenate([packed] * (height // sub), axis=0)

    def chunk(number, _):
        @pl.when(busy[number] != 0)
        def _():
            first = pl.multiple_of(number * CHUNK, CHUNK)
            accounts_now = account[pl.ds(first, CHUNK), :]
            low = (accounts_now & (LOW - 1)).astype(jnp.float32)
            high = accounts_now // LOW
            values = value[pl.ds(first, CHUNK), :]
            bounds = jnp.transpose(threshold[pl.ds(first, CHUNK), :].astype(jnp.float32))
            ratios = ratio[pl.ds(first, CHUNK), :]
            parts = [jnp.where(high == h, values, 0.0) for h in range(high_count)]
            for i in range(CHUNK):
                left, right = scratch[i // half * 2 : i // half * 2 + 2]
                cells = slice(i % half * tile, (i % half + 1) * tile)
                hit = rowed(low[i : i + 1], LOW) == low_id
                for h in range(high_count):
                    left[h * LOW : (h + 1) * LOW, cells] = jnp.where(
                        hit, rowed(parts[h][i : i + 1], LOW), jnp.zeros((), jnp.bfloat16)
                    )
                bound = jnp.broadcast_to(bounds[:, i : i + 1], (tile, bins)).astype(jnp.bfloat16)
                right[cells, :] = jnp.where(
                    bin_id >= bound, rowed(ratios[i : i + 1], tile), jnp.zeros((), jnp.bfloat16)
                )
            for n in range(halves):
                total[...] += jnp.dot(
                    scratch[2 * n][...], scratch[2 * n + 1][...], preferred_element_type=jnp.float32
                )

        return 0

    lax.fori_loop(0, slots // CHUNK, chunk, 0)


def per_device(
    level_start,
    bed_depth,
    wet_bits,
    tile_owner,
    vuln_weight,
    vuln_bias,
    account_index,
    bin_index,
    exposure_value,
    deductible,
    limit,
):
    _, rows, width = level_start.shape
    tile_cells, bin_count = vuln_weight.shape
    account_count = deductible.shape[0]
    owners = lax.axis_size("terrain")
    events = lax.axis_size("event")
    slot_count = account_index.shape[0]
    capacity = slot_count // owners
    share_rows = account_count // owners
    blocks = width // tile_cells
    tiles = rows * blocks

    fields = [level_start[0], bed_depth, wet_bits[0]]
    edges = halos(fields, 4)
    owner = tile_owner[:, 0].reshape(rows, blocks).T.reshape(1, tiles)
    level, outgoing = pl.pallas_call(
        functools.partial(flood_kernel, rows, slot_count, capacity),
        out_shape=(
            jax.ShapeDtypeStruct((rows, width), jnp.float32),
            jax.ShapeDtypeStruct((slot_count, bin_count), jnp.bfloat16),
        ),
        in_specs=[VMEM] * 12,
        out_specs=(VMEM, VMEM),
        name="flood",
    )(
        *fields, *edges, owner, vuln_weight, vuln_bias[None, :],
    )
    outgoing = outgoing.reshape(owners, capacity, bin_count)
    (ratio,) = exchange([outgoing], [("terrain", False)], 1)
    ratio = ratio.reshape(slot_count, bin_count)
    busy = jnp.any(ratio.reshape(slot_count // CHUNK, -1) != 0, axis=1).astype(jnp.int32)
    total = pl.pallas_call(
        loss_kernel,
        out_shape=jax.ShapeDtypeStruct((account_count, bin_count), jnp.float32),
        in_specs=[SMEM] + [VMEM] * 4,
        out_specs=VMEM,
        scratch_shapes=[
            pltpu.VMEM((slot_count, bin_count), jnp.float32),
            pltpu.VMEM((slot_count, tile_cells), jnp.float32),
        ]
        + [
            pltpu.VMEM((account_count, CHUNK // HALVES * tile_cells), jnp.bfloat16),
            pltpu.VMEM((CHUNK // HALVES * tile_cells, bin_count), jnp.bfloat16),
        ]
        * HALVES,
        name="losses",
    )(busy, ratio, account_index, bin_index, exposure_value)
    (parts,) = exchange(
        [total.reshape(owners, share_rows, bin_count)], [("terrain", False)], 2
    )
    scale = account_count / (rows * width * owners)
    net_loss, portfolio = settle(parts, deductible[None, :], limit[None, :], scale, 3)
    portfolio = portfolio.reshape(share_rows, bin_count)
    return (level[None], net_loss.reshape(1, account_count, bin_count), portfolio)


def solution(mesh):
    placed = (
        P("event", "terrain", None),
        P("terrain", None),
        P("event", "terrain", None),
        P("terrain", None),
        P(),
        P(),
        P("terrain", None),
        P("terrain", None),
        P("terrain", None),
        P(),
        P(),
    )
    return jax.shard_map(
        per_device,
        mesh=mesh,
        in_specs=placed,
        out_specs=(P("event", "terrain", None), P("event", None, None), P("terrain", None)),
        check_vma=False,
    )
```

profile of v0, /device:TPU:0, one launch (start us, length us, event | category | flops | bytes accessed | tf_op | source)
XLA Modules:
  0.0 105.7 jit_solution(11128870699274940061)
XLA Ops:
  0.6 0.0 copy-start.1
  0.6 0.5 broadcast.4
  1.2 0.2 copy-done.1
  1.3 0.7 reduce.5
  2.0 0.1 reshape_squeeze.3
  2.1 0.1 copy.15
  2.1 0.7 reshape.25.owner_row
  2.8 9.0 %halos.1 = (f32[8,1024]{1,0:T(8,128)}, f32[8,1024]{1,0:T(8,128)}, s32[8,1024]{1,0:T(8,128)}, f32[8,1024]{1,0:T(8,128)}, f32[8,1024]{1,0:T(8,128)}, /*index=5*/s32[8,1024]{1,0:T(8,128)}) custom-call(f32[32,1024]{1,0:T(8,128)} %bitcast.15, f32[32,1024]{1,0:T(8,128)} %bed_here.1, s32[32,1024]{1,0:T(8,128)} %bitcast.17), custom_call_target="tpu_custom_call" | custom-call | tf_op jit(solution)/shard_map/halos/pallas_call | solution.py:115
  11.8 5.4 %flood.1 = (f32[32,1024]{1,0:T(8,128)}, bf16[384,256]{1,0:T(8,128)(2,1)}) custom-call(f32[32,1024]{1,0:T(8,128)} %bitcast.16, f32[32,1024]{1,0:T(8,128)} %bed_here.1, s32[32,1024]{1,0:T(8,128)} %bitcast.18, f32[8,1024]{1,0:T(8,128)} %get-tuple-element.13.level_above, f32[8,1024]{1,0:T(8,128)} %get-tuple-element.14.bed_above, ...), custom_call_target="tpu_custom_call" | custom-call | tf_op jit(solution)/shard_map/flood/pallas_call | solution.py:396
  17.2 7.1 %exchange1.1 = bf16[8,48,256]{2,1,0:T(8,128)(2,1)} custom-call(bf16[8,48,256]{2,1,0:T(8,128)(2,1)} %bitcast.20), custom_call_target="tpu_custom_call" | custom-call | tf_op jit(solution)/shard_map/exchange1/pallas_call | solution.py:73
  24.3 1.1 %compare_reduce_fusion = pred[8,48]{1,0:T(8,128)(4,1)S(1)} fusion(bf16[8,48,256]{2,1,0:T(8,128)(2,1)} %exchange1.1), kind=kLoop, calls=%fused_computation | loop fusion | flops 196224 | bytes 196992 | tf_op jit(solution)/shard_map/reduce_or | solution.py:411
  25.4 0.1 reduce_or.14
  25.5 0.1 reduce_or.18
  25.7 0.5 convert_element_type.3.busy
  26.2 45.1 %losses.1 = f32[1024,256]{1,0:T(8,128)} custom-call(s32[48]{0:T(128)} %convert_element_type.3.busy, bf16[384,256]{1,0:T(8,128)(2,1)} %bitcast.14, s32[384,128]{1,0:T(8,128)} %account.1, s32[384,128]{1,0:T(8,128)} %threshold.1, bf16[384,128]{1,0:T(8,128)(2,1)} %value_in.1), custom_call_target="tpu_custom_call" | custom-call | tf_op jit(solution)/shard_map/losses/pallas_call | solution.py:412
  71.3 16.6 %exchange2.1.parts = f32[8,128,256]{2,1,0:T(8,128)} custom-call(f32[8,128,256]{2,1,0:T(8,128)} %bitcast.13), custom_call_target="tpu_custom_call" | custom-call | tf_op jit(solution)/shard_map/exchange2/pallas_call | solution.py:73
  87.8 15.3 %settle.1 = (bf16[8,128,256]{2,1,0:T(8,128)(2,1)}, f32[4,32,256]{2,1,0:T(8,128)}) custom-call(f32[8,128,256]{2,1,0:T(8,128)} %exchange2.1.parts, f32[1,1024]{1,0:T(1,128)} %bitcast.23, f32[1,1024]{1,0:T(1,128)} %bitcast.24), custom_call_target="tpu_custom_call" | custom-call | tf_op jit(solution)/shard_map/settle/pallas_call | solution.py:206
  103.2 0.0 copy-start
  103.2 1.9 %copy.18 = bf16[1,1024,256]{2,1,0:T(8,128)(2,1)} copy(bf16[1,1024,256]{2,1,0:T(8,128)(2,1)} %bitcast.19) | data formatting | bytes 1048576
  105.1 0.0 copy-done
  105.1 0.7 copy.19
Async XLA Ops:
  0.6 0.7 copy-start.1
  103.2 1.9 %copy-start = (f32[4,32,256]{2,1,0:T(8,128)S(1)}, f32[4,32,256]{2,1,0:T(8,128)}, u32[]{:S(2)}) copy-start(f32[4,32,256]{2,1,0:T(8,128)} %get-tuple-element.22) | copy-start | bytes 393220
where the time goes:
time: 106 us
  Pallas kernels  98.5 us (93%)
  local copies, waits for them, and re-layouts  4.13 us (4%)
  other arithmetic  2.45 us (2%)
    pallas_call x1, Pallas kernels, per_device(): pl.pallas_call(loss_kernel, out_shape=jax.ShapeDtypeStruct((account_count...  45.1 us
    pallas_call x2, Pallas kernels, exchange(): pl.pallas_call(functools.partial(exchange_kernel, jobs), out_shape=shapes...  23.6 us
    pallas_call x1, Pallas kernels, settle(): pl.pallas_call(functools.partial(settle_kernel, scale), out_shape=(jax.Sh...  15.3 us
    pallas_call x1, Pallas kernels, halos(): pl.pallas_call(halo_kernel, out_shape=shapes, in_specs=[VMEM] * len(field...  9.01 us
    pallas_call x1, Pallas kernels, per_device(): pl.pallas_call(functools.partial(flood_kernel, rows, slot_count, capacity...  5.41 us
    unnamed x7, local copies, waits for them, and re-layouts  3.23 us

commit v1 on v0

v1 whole, which is shorter than its diff:
```python
import functools

import jax
import jax.numpy as jnp
from jax import lax
from jax.experimental import pallas as pl
from jax.experimental.pallas import tpu as pltpu
from jax.sharding import PartitionSpec as P

SUBSTEPS = 8
CHUNK = 8
HALVES = 2
GROUPS = 4

courant = 0.5
gravity = 1.0

VMEM = pl.BlockSpec(memory_space=pltpu.VMEM)
SMEM = pl.BlockSpec(memory_space=pltpu.SMEM)
MESH = pl.DeviceIdType.MESH


def exchange_kernel(jobs, *refs):
    count = len(jobs)
    sources, targets, sems = refs[:count], refs[count : 2 * count], refs[2 * count :]
    barrier = pltpu.get_barrier_semaphore()
    greeted = 0
    for axis in dict.fromkeys(axis for axis, _ in jobs):
        size = lax.axis_size(axis)
        me = lax.axis_index(axis)
        for hop in range(1, size):
            pl.semaphore_signal(
                barrier, inc=1, device_id={axis: lax.rem(me + hop, size)}, device_id_type=MESH
            )
        greeted += size - 1
    pl.semaphore_wait(barrier, greeted)
    copies = []
    for job, (axis, spread) in enumerate(jobs):
        source, target = sources[job], targets[job]
        local, sent, received = sems[3 * job : 3 * job + 3]
        size = lax.axis_size(axis)
        me = lax.axis_index(axis)
        for hop in range(1, size):
            peer = lax.rem(me + hop, size)
            copy = pltpu.make_async_remote_copy(
                src_ref=source if spread else source.at[peer],
                dst_ref=target.at[me],
                send_sem=sent.at[hop],
                recv_sem=received.at[hop],
                device_id={axis: peer},
                device_id_type=MESH,
            )
            copy.start()
            copies.append(copy)
        own = pltpu.make_async_copy(source if spread else source.at[me], target.at[me], local)
        own.start()
        copies.append(own)
    for copy in copies:
        copy.wait()


def exchange(arrays, jobs, number):
    shapes, scratch = [], []
    for array, (axis, spread) in zip(arrays, jobs):
        size = lax.axis_size(axis)
        shape = (size,) + array.shape if spread else array.shape
        shapes.append(jax.ShapeDtypeStruct(shape, array.dtype))
        scratch += [
            pltpu.SemaphoreType.DMA,
            pltpu.SemaphoreType.DMA((size,)),
            pltpu.SemaphoreType.DMA((size,)),
        ]
    return pl.pallas_call(
        functools.partial(exchange_kernel, jobs),
        out_shape=shapes,
        in_specs=[VMEM] * len(arrays),
        out_specs=[VMEM] * len(arrays),
        scratch_shapes=scratch,
        compiler_params=pltpu.CompilerParams(collective_id=number, has_side_effects=True),
        name="exchange" + str(number),
    )(*arrays)


def settle_kernel(
    scale, parts, floor, roof, net_loss, portfolio,
    made, made_low, kept, kept_low, arrived, summed, kept_sum, local,
    sent_low, got_low, sent_net, got_net, sent_sum, got_sum,
):
    owners, share_rows, _ = parts.shape
    events = lax.axis_size("event")
    me, group = lax.axis_index("terrain"), lax.axis_index("event")
    barrier = pltpu.get_barrier_semaphore()
    for axis, size, mine in (("terrain", owners, me), ("event", events, group)):
        for hop in range(1, size):
            pl.semaphore_signal(
                barrier, inc=1, device_id={axis: lax.rem(mine + hop, size)}, device_id_type=MESH
            )
    whole = parts[0]
    for n in range(1, owners):
        whole = whole + parts[n]
    picked = (share_rows, floor.shape[1])
    account = lax.broadcasted_iota(jnp.int32, picked, 1)
    mine = account == lax.broadcasted_iota(jnp.int32, picked, 0) + me * share_rows

    def of_share(terms):
        return jnp.sum(jnp.where(mine, terms[...], 0.0), axis=1, keepdims=True)

    net = jnp.minimum(jnp.maximum(whole * scale - of_share(floor), 0.0), of_share(roof))
    made[...] = net.reshape(made.shape)
    made_low[...] = net.astype(made_low.dtype)
    first = [
        pltpu.make_async_copy(made, kept, local.at[0]),
        pltpu.make_async_copy(made_low, kept_low, local.at[1]),
    ]
    for copy in first:
        copy.start()
    pl.semaphore_wait(barrier, owners + events - 2)
    for copy in first:
        copy.wait()

    def push(axis, size, index, source, target, sent, received, split):
        copies = []
        for hop in range(1, size):
            peer = lax.rem(index + hop, size)
            copy = pltpu.make_async_remote_copy(
                src_ref=source.at[peer] if split else source,
                dst_ref=target.at[index],
                send_sem=sent.at[hop],
                recv_sem=received.at[hop],
                device_id={axis: peer},
                device_id_type=MESH,
            )
            copy.start()
            copies.append(copy)
        return copies

    nets = push("event", events, group, kept, arrived, sent_net, got_net, True)
    own_net = pltpu.make_async_copy(kept.at[group], arrived.at[group], local.at[2])
    own_net.start()
    lows = push("terrain", owners, me, kept_low, net_loss, sent_low, got_low, False)
    own_low = pltpu.make_async_copy(kept_low, net_loss.at[me], local.at[3])
    own_low.start()
    for copy in nets + [own_net]:
        copy.wait()
    total = arrived[0]
    for n in range(1, events):
        total = total + arrived[n]
    summed[...] = total / events
    last = pltpu.make_async_copy(summed, kept_sum, local.at[4])
    last.start()
    last.wait()
    sums = push("event", events, group, kept_sum, portfolio, sent_sum, got_sum, False)
    own_sum = pltpu.make_async_copy(kept_sum, portfolio.at[group], local.at[5])
    own_sum.start()
    for copy in sums + [own_sum] + lows + [own_low]:
        copy.wait()


def settle(parts, floor, roof, scale, number):
    owners, share_rows, bins = parts.shape
    events = lax.axis_size("event")
    split = (events, share_rows // events, bins)
    dma = pltpu.SemaphoreType.DMA
    return pl.pallas_call(
        functools.partial(settle_kernel, scale),
        out_shape=(
            jax.ShapeDtypeStruct((owners, share_rows, bins), jnp.bfloat16),
            jax.ShapeDtypeStruct(split, jnp.float32),
        ),
        in_specs=[VMEM] * 3,
        out_specs=(VMEM, VMEM),
        scratch_shapes=[
            pltpu.VMEM(split, jnp.float32),
            pltpu.VMEM((share_rows, bins), jnp.bfloat16),
            pltpu.VMEM(split, jnp.float32),
            pltpu.VMEM((share_rows, bins), jnp.bfloat16),
            pltpu.VMEM(split, jnp.float32),
            pltpu.VMEM(split[1:], jnp.float32),
            pltpu.VMEM(split[1:], jnp.float32),
            dma((6,)),
        ]
        + [dma((owners,))] * 2
        + [dma((events,))] * 4,
        compiler_params=pltpu.CompilerParams(collective_id=number, has_side_effects=True),
        name="settle",
    )(parts, floor, roof)


def padded(count, unit):
    return -(-count // unit) * unit


def front_kernel(
    level_here, bed_here, wet_here, account, threshold, value, owner_row, weight, bias,
    level_out, ratio_out, low_out, bin_out, value_out,
    made, kept, got, level_above, bed_above, wet_above, level_below, bed_below, wet_below,
    halo_sent, halo_got, cell_sent, cell_got, local,
):
    size = lax.axis_size("terrain")
    me = lax.axis_index("terrain")
    barrier = pltpu.get_barrier_semaphore()
    for hop in range(1, size):
        pl.semaphore_signal(
            barrier, inc=1, device_id={"terrain": lax.rem(me + hop, size)}, device_id_type=MESH
        )
    rows, width = level_here.shape
    capacity = account.shape[0] // size
    room = made.shape[2]

    accounts = account[...]
    low = (accounts & 255) - ((accounts >> 8) & 1) * 256
    bound = threshold[...] - (accounts >> 9) * 256
    fields = (low.astype(jnp.float32), bound.astype(jnp.float32), value[...].astype(jnp.float32))
    if room != capacity:
        made[...] = jnp.zeros(made.shape, made.dtype)
    for n in range(size):
        for f in range(3):
            made[n, f, :capacity, :] = fields[f][n * capacity : (n + 1) * capacity].astype(
                made.dtype
            )
    keep = pltpu.make_async_copy(made, kept, local.at[0])
    keep.start()
    pl.semaphore_wait(barrier, size - 1)

    later, earlier = lax.rem(me + 1, size), lax.rem(me + size - 1, size)
    strips = (level_here, bed_here, wet_here)
    above = (level_above, bed_above, wet_above)
    below = (level_below, bed_below, wet_below)
    edges = []
    for side, (peer, targets) in enumerate(((later, above), (earlier, below))):
        for i in range(3):
            first = 0 if side else rows - SUBSTEPS
            copy = pltpu.make_async_remote_copy(
                src_ref=strips[i].at[pl.ds(first, SUBSTEPS)],
                dst_ref=targets[i],
                send_sem=halo_sent.at[side * 3 + i],
                recv_sem=halo_got.at[side * 3 + i],
                device_id={"terrain": peer},
                device_id_type=MESH,
            )
            copy.start()
            edges.append(copy)
    keep.wait()
    cells = []
    for hop in range(1, size):
        peer = lax.rem(me + hop, size)
        copy = pltpu.make_async_remote_copy(
            src_ref=kept.at[peer],
            dst_ref=got.at[me],
            send_sem=cell_sent.at[hop],
            recv_sem=cell_got.at[hop],
            device_id={"terrain": peer},
            device_id_type=MESH,
        )
        copy.start()
        cells.append(copy)
    own = pltpu.make_async_copy(kept.at[me], got.at[me], local.at[1])
    own.start()
    cells.append(own)

    tile = weight.shape[0]
    blocks = width // tile
    tiles = rows * blocks
    number = lax.broadcasted_iota(jnp.int32, (tiles, tiles), 0)
    number = (number % rows) * blocks + number // rows
    along = lax.broadcasted_iota(jnp.int32, (tiles, tiles), 1)
    owner = owner_row[...].astype(jnp.float32)
    owner_column = jnp.sum(jnp.where(along == number, owner, 0.0), axis=1, keepdims=True)
    same = (owner_column == owner) & (along < number)
    rank = jnp.sum(jnp.where(same, 1.0, 0.0), axis=1, keepdims=True)
    slot = lax.broadcasted_iota(jnp.int32, (tiles, size * room), 1).astype(jnp.float32)
    chosen = jnp.where(slot == owner_column * room + rank, 1.0, 0.0).astype(jnp.bfloat16)

    for copy in edges:
        copy.wait()
    first_row = me * rows - SUBSTEPS
    total_rows = rows * size
    level = jnp.concatenate([level_above[...], level_here[...], level_below[...]], axis=0)
    bed = jnp.concatenate([bed_above[...], bed_here[...], bed_below[...]], axis=0)
    wet = jnp.concatenate([wet_above[...], wet_here[...], wet_below[...]], axis=0)
    shape = level.shape
    tall = shape[0]
    row_id = first_row + lax.broadcasted_iota(jnp.int32, shape, 0)
    column = lax.broadcasted_iota(jnp.int32, shape, 1)
    inside = ((row_id >= 0) & (row_id < total_rows)).astype(jnp.float32)
    not_first = (column > 0).astype(jnp.float32)
    not_last = (column < width - 1).astype(jnp.float32)

    def down(field):
        return pltpu.roll(field, tall - 1, 0)

    def up(field):
        return pltpu.roll(field, 1, 0)

    def right(field):
        return pltpu.roll(field, width - 1, 1) * not_last

    def left(field):
        return pltpu.roll(field, 1, 1) * not_first

    quarter = 0.25
    assert courant * gravity == 0.5
    level = level * inside
    row_speed = jnp.zeros(shape, jnp.float32)
    col_speed = jnp.zeros(shape, jnp.float32)
    for step in range(SUBSTEPS):
        wet_factor = ((wet >> step) & 1).astype(jnp.float32) * (inside * quarter)
        if step:
            row_flow, col_flow = bed * row_speed, bed * col_speed
            new_level = (
                down(level - row_flow) + up(level + row_flow)
                + (right(level - col_flow) + left(level + col_flow))
            )
            new_row = (
                down(row_speed - level) + up(row_speed + level)
                + (right(row_speed) + left(row_speed))
            )
            new_col = (
                down(col_speed) + up(col_speed)
                + (right(col_speed - level) + left(col_speed + level))
            )
            row_speed, col_speed = new_row * wet_factor, new_col * wet_factor
        else:
            ld, lu, lr, ll = down(level), up(level), right(level), left(level)
            new_level = ld + lu + (lr + ll)
            row_speed = (lu - ld) * wet_factor
            col_speed = (ll - lr) * wet_factor
        level = new_level * (inside * quarter)
    level = level[SUBSTEPS : SUBSTEPS + rows]
    level_out[...] = level
    pieces = jnp.concatenate(
        [level[:, j * tile : (j + 1) * tile] for j in range(blocks)], axis=0
    ).astype(jnp.bfloat16)
    ratio_out[...] = jax.nn.sigmoid(
        jnp.dot(pieces, weight[...], preferred_element_type=jnp.float32) + bias[...]
    ).astype(jnp.bfloat16)
    for copy in cells:
        copy.wait()
    for f, target in enumerate((low_out, bin_out, value_out)):
        records = jnp.concatenate([got[n, f] for n in range(size)], axis=0)
        target[...] = jnp.dot(chosen, records, preferred_element_type=jnp.float32).astype(
            target.dtype
        )


def front(strips, records, owner_row, weight, bias, number):
    rows, width = strips[0].shape
    slots, cells = records[0].shape
    size = lax.axis_size("terrain")
    tiles = rows * width // cells
    packed = (size, 3, padded(slots // size, 16), cells)
    edge = (SUBSTEPS, width)
    dma = pltpu.SemaphoreType.DMA
    edges = [pltpu.VMEM(edge, f.dtype) for f in strips]
    return pl.pallas_call(
        front_kernel,
        out_shape=(
            jax.ShapeDtypeStruct((rows, width), jnp.float32),
            jax.ShapeDtypeStruct((tiles, weight.shape[1]), jnp.bfloat16),
        )
        + (jax.ShapeDtypeStruct((tiles, cells), jnp.bfloat16),) * 3,
        in_specs=[VMEM] * 9,
        out_specs=(VMEM,) * 5,
        scratch_shapes=[pltpu.VMEM(packed, jnp.bfloat16)] * 3
        + edges * 2
        + [dma((6,))] * 2
        + [dma((size,))] * 2
        + [dma((2,))],
        compiler_params=pltpu.CompilerParams(collective_id=number, has_side_effects=True),
        name="front",
    )(*strips, *records, owner_row, weight, bias)


def rowed(row, height):
    packed = jnp.broadcast_to(row, (16, row.shape[1])).astype(jnp.bfloat16)
    return jnp.concatenate([packed] * (height // 16), axis=0)


def numbered(height, width, axis):
    return (
        lax.broadcasted_iota(jnp.int32, (height, width), axis)
        .astype(jnp.float32)
        .astype(jnp.bfloat16)
    )


def loss_kernel(
    low_in, bin_in, value_in, ratio_in, total,
    ratio, meta, places, lows, bounds, values, *halves,
):
    accounts, bins = total.shape
    tiles, cells = low_in.shape
    groups = lows.shape[0]
    group_size = accounts // groups
    capacity = 2 * cells // groups
    together = cells // capacity
    bundles = tiles // together
    zero = jnp.zeros((), jnp.bfloat16)
    one = jnp.ones((), jnp.bfloat16)

    low = low_in[...].astype(jnp.float32)
    bound = bin_in[...].astype(jnp.float32)
    high = jnp.where(low < 0, 1, 0) + jnp.where(bound < 0, 2, 0)
    low = jnp.where(low < 0, low + 256.0, low).astype(jnp.int32) + high * 256
    bound = jnp.where(bound < 0, bound + 256.0, bound)
    group = low // group_size
    low = low % group_size
    value = value_in[...].astype(jnp.float32)
    ratio[...] = ratio_in[...].astype(jnp.float32)
    earlier = jnp.where(
        lax.broadcasted_iota(jnp.int32, (cells, cells), 0)
        < lax.broadcasted_iota(jnp.int32, (cells, cells), 1),
        1.0,
        0.0,
    ).astype(jnp.bfloat16)
    turn = lax.broadcasted_iota(jnp.int32, (tiles, cells), 0) % together
    rank = jnp.zeros((tiles, cells), jnp.float32)
    for h in range(groups):
        mine = group == h
        count = jnp.dot(
            jnp.where(mine, 1.0, 0.0).astype(jnp.bfloat16),
            earlier,
            preferred_element_type=jnp.float32,
        )
        rank = jnp.where(mine, count, rank)
    base = (group // together) * cells + ((group + turn) % together) * capacity
    fits = rank < capacity
    places[...] = jnp.where(fits, base.astype(jnp.float32) + rank, -1.0)
    meta[:, 0, :] = low.astype(jnp.float32)
    meta[:, 1, :] = bound
    meta[:, 2, :] = value
    meta[:, 3, :] = group.astype(jnp.float32)
    spilled = jnp.max(rank) >= capacity

    place_id = numbered(2 * cells, cells, 0)
    lane = lax.broadcasted_iota(jnp.int32, (8, cells), 1) // capacity

    def gather(bundle, _):
        found = []
        for j in range(together):
            t = bundle * together + j
            here = rowed(places[pl.ds(t, 1), :], 2 * cells) == place_id
            found.append(
                lax.dot_general(
                    meta[t].astype(jnp.bfloat16),
                    jnp.where(here, one, zero),
                    (((1,), (1,)), ((), ())),
                    preferred_element_type=jnp.float32,
                )
            )
        for q in range(2):
            parts = [f[:, q * cells : (q + 1) * cells] for f in found]
            for r in range(together):
                mixed = parts[(0 - r) % together]
                for e in range(1, together):
                    mixed = jnp.where(lane == e, parts[(e - r) % together], mixed)
                h = q * together + r
                lows[h, pl.ds(bundle, 1), :] = mixed[0:1]
                bounds[h, pl.ds(bundle, 1), :] = mixed[1:2]
                values[h, pl.ds(bundle, 1), :] = mixed[2:3]
        return 0

    lax.fori_loop(0, bundles, gather, 0)

    total[...] = jnp.zeros(total.shape, jnp.float32)
    account_id = numbered(group_size, cells, 0)
    bin_row = numbered(16, bins, 1)
    bin_id = jnp.concatenate([bin_row] * (cells // 16), axis=0)
    count = len(halves) // 2
    half = halves[1].shape[0] // cells

    for h in range(groups):
        rows = pl.ds(h * group_size, group_size)

        def chunk(number, _):
            first = pl.multiple_of(number * CHUNK, CHUNK)
            first_tile = pl.multiple_of(number * CHUNK * together, CHUNK * together)
            low_rows = lows[h, pl.ds(first, CHUNK), :]
            value_rows = values[h, pl.ds(first, CHUNK), :]
            columns = jnp.transpose(bounds[h, pl.ds(first, CHUNK), :])
            ratios = ratio[pl.ds(first_tile, CHUNK * together), :]
            for i in range(CHUNK):
                left, right = halves[i // half * 2 : i // half * 2 + 2]
                spot = slice(i % half * cells, (i % half + 1) * cells)
                left[:, spot] = jnp.where(
                    rowed(low_rows[i : i + 1], group_size) == account_id,
                    rowed(value_rows[i : i + 1], group_size),
                    zero,
                )
                bound = jnp.broadcast_to(columns[:, i : i + 1], (cells, bins)).astype(jnp.bfloat16)
                shown = []
                for e in range(together):
                    t = i * together + (e - h) % together
                    shown.append(rowed(ratios[t : t + 1], capacity))
                right[spot, :] = jnp.where(
                    bin_id >= bound, jnp.concatenate(shown, axis=0), zero
                )
            for n in range(count):
                total[rows, :] += jnp.dot(
                    halves[2 * n][...], halves[2 * n + 1][...], preferred_element_type=jnp.float32
                )
            return 0

        lax.fori_loop(0, bundles // CHUNK, chunk, 0)

    @pl.when(spilled)
    def _():
        def dense(t, _):
            fields = meta[t]
            rest = jnp.where(places[pl.ds(t, 1), :] < 0, fields[2:3], 0.0)

            @pl.when(jnp.max(rest) > 0)
            def _():
                hit = rowed(fields[0:1], group_size) == account_id
                column = jnp.transpose(fields)[:, 1:2]
                bound = jnp.broadcast_to(column, (cells, bins)).astype(jnp.bfloat16)
                right = jnp.where(bin_id >= bound, rowed(ratio[pl.ds(t, 1), :], cells), zero)
                for h in range(groups):
                    part = jnp.where(fields[3:4] == h, rest, 0.0)
                    left = jnp.where(hit, rowed(part, group_size), zero)
                    total[pl.ds(h * group_size, group_size), :] += jnp.dot(
                        left, right, preferred_element_type=jnp.float32
                    )

            return 0

        lax.fori_loop(0, tiles, dense, 0)


def losses(low, bound, value, ratio, account_count):
    tiles, cells = low.shape
    bins = ratio.shape[1]
    groups = GROUPS
    together = groups // 2
    gathered = pltpu.VMEM((groups, tiles // together, cells), jnp.float32)
    return pl.pallas_call(
        loss_kernel,
        out_shape=jax.ShapeDtypeStruct((account_count, bins), jnp.float32),
        in_specs=[VMEM] * 4,
        out_specs=VMEM,
        scratch_shapes=[
            pltpu.VMEM((tiles, bins), jnp.float32),
            pltpu.VMEM((tiles, 8, cells), jnp.float32),
            pltpu.VMEM((tiles, cells), jnp.float32),
            gathered, gathered, gathered,
        ]
        + [
            pltpu.VMEM((account_count // groups, CHUNK // HALVES * cells), jnp.bfloat16),
            pltpu.VMEM((CHUNK // HALVES * cells, bins), jnp.bfloat16),
        ]
        * HALVES,
        name="losses",
    )(low, bound, value, ratio)


def per_device(
    level_start,
    bed_depth,
    wet_bits,
    tile_owner,
    vuln_weight,
    vuln_bias,
    account_index,
    bin_index,
    exposure_value,
    deductible,
    limit,
):
    _, rows, width = level_start.shape
    tile_cells, bin_count = vuln_weight.shape
    account_count = deductible.shape[0]
    owners = lax.axis_size("terrain")
    events = lax.axis_size("event")
    share_rows = account_count // owners
    tiles = rows * width // tile_cells
    level, ratio, low, bound, value = front(
        [level_start[0], bed_depth, wet_bits[0]],
        [account_index, bin_index, exposure_value],
        tile_owner.reshape(1, tiles),
        vuln_weight,
        vuln_bias[None, :],
        1,
    )
    total = losses(low, bound, value, ratio, account_count)
    (parts,) = exchange(
        [total.reshape(owners, share_rows, bin_count)], [("terrain", False)], 2
    )
    scale = account_count / (rows * width * owners)
    net_loss, portfolio = settle(parts, deductible[None, :], limit[None, :], scale, 3)
    portfolio = portfolio.reshape(share_rows, bin_count)
    return (level[None], net_loss.reshape(1, account_count, bin_count), portfolio)


def solution(mesh):
    placed = (
        P("event", "terrain", None),
        P("terrain", None),
        P("event", "terrain", None),
        P("terrain", None),
        P(),
        P(),
        P("terrain", None),
        P("terrain", None),
        P("terrain", None),
        P(),
        P(),
    )
    return jax.shard_map(
        per_device,
        mesh=mesh,
        in_specs=placed,
        out_specs=(P("event", "terrain", None), P("event", None, None), P("terrain", None)),
        check_vma=False,
    )
```

time: 106 us -> 104 us (0.981)
  other arithmetic: 2.45 us -> 0 us
  Pallas kernels: 98.5 us -> 99.7 us
    pallas_call x3 -> x2, Pallas kernels: 59.5 us -> 67.4 us  [the longest x1 54.6 us: losses(): pl.pallas_call(loss_kernel, out_shape=jax.ShapeDtypeStruct((account_count...]
    pallas_call x2 -> x1, Pallas kernels: 23.6 us -> 16.6 us  [exchange(): pl.pallas_call(functools.partial(exchange_kernel, jobs), out_shape=shapes...]
    reduce_or x2 -> x0, other arithmetic: 1.26 us -> none  [per_device(): jnp.any(ratio.reshape(slot_count // CHUNK, -1) != 0, axis=1)]
where the time goes in v1:
time: 104 us
  Pallas kernels  99.7 us (96%)
  local copies, waits for them, and re-layouts  3.22 us (3%)
    pallas_call x1, Pallas kernels, losses(): pl.pallas_call(loss_kernel, out_shape=jax.ShapeDtypeStruct((account_count...  54.6 us
    pallas_call x1, Pallas kernels, exchange(): pl.pallas_call(functools.partial(exchange_kernel, jobs), out_shape=shapes...  16.6 us
    pallas_call x1, Pallas kernels, settle(): pl.pallas_call(functools.partial(settle_kernel, scale), out_shape=(jax.Sh...  15.7 us
    pallas_call x1, Pallas kernels, front(): pl.pallas_call(front_kernel, out_shape=(jax.ShapeDtypeStruct((rows, width...  12.8 us
    unnamed x7, local copies, waits for them, and re-layouts  3.22 us

profile of v1, /device:TPU:0, one launch (start us, length us, event | category | flops | bytes accessed | tf_op | source)
XLA Modules:
  0.0 103.6 jit_solution(15042869020792375313)
XLA Ops:
  0.6 12.8 %front.1 = (f32[32,1024]{1,0:T(8,128)}, bf16[256,256]{1,0:T(8,128)(2,1)}, bf16[256,128]{1,0:T(8,128)(2,1)}, bf16[256,128]{1,0:T(8,128)(2,1)}, bf16[256,128]{1,0:T(8,128)(2,1)}) custom-call(f32[32,1024]{1,0:T(8,128)} %bitcast.14, f32[32,1024]{1,0:T(8,128)} %bed_here.1, s32[32,1024]{1,0:T(8,128)} %bitcast.15, s32[384,128]{1,0:T(8,128)} %account.1, ...), custom_call_target="tpu_custom_call" | custom-call | tf_op jit(solution)/shard_map/front/pallas_call | solution.py:355
  13.5 54.6 %losses.1 = f32[1024,256]{1,0:T(8,128)} custom-call(bf16[256,128]{1,0:T(8,128)(2,1)} %get-tuple-element.11.low_in, bf16[256,128]{1,0:T(8,128)(2,1)} %get-tuple-element.12.bin_in, bf16[256,128]{1,0:T(8,128)(2,1)} %get-tuple-element.13.value_in, bf16[256,256]{1,0:T(8,128)(2,1)} %get-tuple-element.14.ratio_in), custom_call_target="tpu_custom_call" | custom-call | tf_op jit(solution)/shard_map/losses/pallas_call | solution.py:536
  68.0 16.6 %exchange2.1.parts = f32[8,128,256]{2,1,0:T(8,128)} custom-call(f32[8,128,256]{2,1,0:T(8,128)} %bitcast.10), custom_call_target="tpu_custom_call" | custom-call | tf_op jit(solution)/shard_map/exchange2/pallas_call | solution.py:73
  84.7 0.0 copy-start
  84.7 15.7 %settle.1 = (bf16[8,128,256]{2,1,0:T(8,128)(2,1)}, f32[4,32,256]{2,1,0:T(8,128)}) custom-call(f32[8,128,256]{2,1,0:T(8,128)} %exchange2.1.parts, f32[1,1024]{1,0:T(1,128)} %bitcast.16, f32[1,1024]{1,0:T(1,128)} %bitcast.17), custom_call_target="tpu_custom_call" | custom-call | tf_op jit(solution)/shard_map/settle/pallas_call | solution.py:164
  100.4 0.0 copy-done
  100.4 0.7 copy.17
  101.1 0.0 copy-start.1
  101.1 1.9 %copy.18 = bf16[1,1024,256]{2,1,0:T(8,128)(2,1)} copy(bf16[1,1024,256]{2,1,0:T(8,128)(2,1)} %bitcast.11) | data formatting | bytes 1048576
  103.0 0.0 copy-done.1
  103.0 0.7 copy.19
Async XLA Ops:
  84.7 15.7 %copy-start = (f32[32,1024]{1,0:T(8,128)S(1)}, f32[32,1024]{1,0:T(8,128)}, u32[]{:S(2)}) copy-start(f32[32,1024]{1,0:T(8,128)} %get-tuple-element.10) | copy-start | bytes 393220
  101.1 1.9 %copy-start.1 = (f32[4,32,256]{2,1,0:T(8,128)S(1)}, f32[4,32,256]{2,1,0:T(8,128)}, u32[]{:S(2)}) copy-start(f32[4,32,256]{2,1,0:T(8,128)} %get-tuple-element.16) | copy-start | bytes 393220

commit v2 on v1

--- a/solution.py
+++ b/solution.py
@@ -9,8 +9,10 @@
 
 SUBSTEPS = 8
 CHUNK = 8
-HALVES = 2
-GROUPS = 4
+GROUPS = 8
+SPAN = 32
+BUFFERS = 2
+UNROLL = 8
 
 courant = 0.5
 gravity = 1.0
@@ -386,7 +388,7 @@
 
 def loss_kernel(
     low_in, bin_in, value_in, ratio_in, total,
-    ratio, meta, places, lows, bounds, values, *halves,
+    ratio, low_all, bound_all, value_all, places, lows, bounds, values, *halves,
 ):
     accounts, bins = total.shape
     tiles, cells = low_in.shape
@@ -400,12 +402,12 @@
 
     low = low_in[...].astype(jnp.float32)
     bound = bin_in[...].astype(jnp.float32)
-    high = jnp.where(low < 0, 1, 0) + jnp.where(bound < 0, 2, 0)
-    low = jnp.where(low < 0, low + 256.0, low).astype(jnp.int32) + high * 256
-    bound = jnp.where(bound < 0, bound + 256.0, bound)
-    group = low // group_size
-    low = low % group_size
-    value = value_in[...].astype(jnp.float32)
+    high = jnp.where(low < 0, 256.0, 0.0) + jnp.where(bound < 0, 512.0, 0.0)
+    low = jnp.where(low < 0, low + 256.0, low) + high
+    group = low.astype(jnp.int32) // group_size
+    low_all[...] = low - (group * group_size).astype(jnp.float32)
+    bound_all[...] = jnp.where(bound < 0, bound + 256.0, bound)
+    value_all[...] = value_in[...].astype(jnp.float32)
     ratio[...] = ratio_in[...].astype(jnp.float32)
     earlier = jnp.where(
         lax.broadcasted_iota(jnp.int32, (cells, cells), 0)
@@ -425,106 +427,115 @@
         rank = jnp.where(mine, count, rank)
     base = (group // together) * cells + ((group + turn) % together) * capacity
     fits = rank < capacity
-    places[...] = jnp.where(fits, base.astype(jnp.float32) + rank, -1.0)
-    meta[:, 0, :] = low.astype(jnp.float32)
-    meta[:, 1, :] = bound
-    meta[:, 2, :] = value
-    meta[:, 3, :] = group.astype(jnp.float32)
-    spilled = jnp.max(rank) >= capacity
+    places[...] = jnp.where(fits, base.astype(jnp.float32) + rank, -1.0 - group.astype(jnp.float32))
 
     place_id = numbered(2 * cells, cells, 0)
     lane = lax.broadcasted_iota(jnp.int32, (8, cells), 1) // capacity
-
-    def gather(bundle, _):
-        found = []
-        for j in range(together):
-            t = bundle * together + j
-            here = rowed(places[pl.ds(t, 1), :], 2 * cells) == place_id
-            found.append(
-                lax.dot_general(
-                    meta[t].astype(jnp.bfloat16),
-                    jnp.where(here, one, zero),
-                    (((1,), (1,)), ((), ())),
-                    preferred_element_type=jnp.float32,
+    field = lax.broadcasted_iota(jnp.int32, (8, cells), 0)
+    unroll = max(1, UNROLL // together)
+
+    def spread(ref, t):
+        return jnp.broadcast_to(ref[pl.ds(t, 1), :], (8, cells))
+
+    def gather(number, _):
+        for u in range(unroll):
+            bundle = number * unroll + u
+            found = []
+            for j in range(together):
+                t = bundle * together + j
+                here = rowed(places[pl.ds(t, 1), :], 2 * cells) == place_id
+                fields = jnp.where(
+                    field == 0,
+                    spread(low_all, t),
+                    jnp.where(field == 1, spread(bound_all, t), spread(value_all, t)),
                 )
-            )
-        for q in range(2):
-            parts = [f[:, q * cells : (q + 1) * cells] for f in found]
-            for r in range(together):
-                mixed = parts[(0 - r) % together]
-                for e in range(1, together):
-                    mixed = jnp.where(lane == e, parts[(e - r) % together], mixed)
-                h = q * together + r
-                lows[h, pl.ds(bundle, 1), :] = mixed[0:1]
-                bounds[h, pl.ds(bundle, 1), :] = mixed[1:2]
-                values[h, pl.ds(bundle, 1), :] = mixed[2:3]
+                found.append(
+                    lax.dot_general(
+                        fields.astype(jnp.bfloat16),
+                        jnp.where(here, one, zero),
+                        (((1,), (1,)), ((), ())),
+                        preferred_element_type=jnp.float32,
+                    )
+                )
+            for q in range(2):
+                parts = [f[:, q * cells : (q + 1) * cells] for f in found]
+                for r in range(together):
+                    mixed = parts[(0 - r) % together]
+                    for e in range(1, together):
+                        mixed = jnp.where(lane == e, parts[(e - r) % together], mixed)
+                    h = q * together + r
+                    lows[h, pl.ds(bundle, 1), :] = mixed[0:1]
+                    bounds[h, pl.ds(bundle, 1), :] = mixed[1:2]
+                    values[h, pl.ds(bundle, 1), :] = mixed[2:3]
         return 0
 
-    lax.fori_loop(0, bundles, gather, 0)
-
-    total[...] = jnp.zeros(total.shape, jnp.float32)
+    lax.fori_loop(0, bundles // unroll, gather, 0)
+
     account_id = numbered(group_size, cells, 0)
-    bin_row = numbered(16, bins, 1)
-    bin_id = jnp.concatenate([bin_row] * (cells // 16), axis=0)
-    count = len(halves) // 2
-    half = halves[1].shape[0] // cells
-
-    for h in range(groups):
-        rows = pl.ds(h * group_size, group_size)
-
-        def chunk(number, _):
-            first = pl.multiple_of(number * CHUNK, CHUNK)
-            first_tile = pl.multiple_of(number * CHUNK * together, CHUNK * together)
-            low_rows = lows[h, pl.ds(first, CHUNK), :]
-            value_rows = values[h, pl.ds(first, CHUNK), :]
-            columns = jnp.transpose(bounds[h, pl.ds(first, CHUNK), :])
-            ratios = ratio[pl.ds(first_tile, CHUNK * together), :]
-            for i in range(CHUNK):
-                left, right = halves[i // half * 2 : i // half * 2 + 2]
-                spot = slice(i % half * cells, (i % half + 1) * cells)
-                left[:, spot] = jnp.where(
-                    rowed(low_rows[i : i + 1], group_size) == account_id,
-                    rowed(value_rows[i : i + 1], group_size),
-                    zero,
-                )
-                bound = jnp.broadcast_to(columns[:, i : i + 1], (cells, bins)).astype(jnp.bfloat16)
-                shown = []
-                for e in range(together):
-                    t = i * together + (e - h) % together
-                    shown.append(rowed(ratios[t : t + 1], capacity))
-                right[spot, :] = jnp.where(
-                    bin_id >= bound, jnp.concatenate(shown, axis=0), zero
-                )
-            for n in range(count):
-                total[rows, :] += jnp.dot(
-                    halves[2 * n][...], halves[2 * n + 1][...], preferred_element_type=jnp.float32
-                )
-            return 0
-
-        lax.fori_loop(0, bundles // CHUNK, chunk, 0)
+    bin_id = jnp.concatenate([numbered(16, bins, 1)] * (cells // 16), axis=0)
+    buffers = len(halves) // 2
+    span = halves[1].shape[0] // cells
+
+    def one_group(h, _):
+        rows = pl.ds(pl.multiple_of(h * group_size, group_size), group_size)
+        summed = None
+        for c in range(bundles // span):
+            left, right = halves[c % buffers * 2 : c % buffers * 2 + 2]
+            for block in range(span // CHUNK):
+                first = c * span + block * CHUNK
+                columns = jnp.transpose(bounds[h, first : first + CHUNK, :]).astype(jnp.bfloat16)
+                for i in range(CHUNK):
+                    bundle = first + i
+                    spot = slice((block * CHUNK + i) * cells, (block * CHUNK + i + 1) * cells)
+                    left[:, spot] = jnp.where(
+                        rowed(lows[h, bundle : bundle + 1, :], group_size) == account_id,
+                        rowed(values[h, bundle : bundle + 1, :], group_size),
+                        zero,
+                    )
+                    shown = []
+                    for e in range(together):
+                        t = bundle * together + lax.rem(e + groups - h, together)
+                        shown.append(rowed(ratio[pl.ds(t, 1), :], capacity))
+                    right[spot, :] = jnp.where(
+                        bin_id >= jnp.broadcast_to(columns[:, i : i + 1], (cells, bins)),
+                        jnp.concatenate(shown, axis=0),
+                        zero,
+                    )
+            part = jnp.dot(left[...], right[...], preferred_element_type=jnp.float32)
+            summed = part if summed is None else summed + part
+        total[rows, :] = summed
+        return 0
+
+    lax.fori_loop(0, groups, one_group, 0)
+
+    spilled = jnp.max(rank) >= capacity
 
     @pl.when(spilled)
     def _():
-        def dense(t, _):
-            fields = meta[t]
-            rest = jnp.where(places[pl.ds(t, 1), :] < 0, fields[2:3], 0.0)
-
-            @pl.when(jnp.max(rest) > 0)
-            def _():
-                hit = rowed(fields[0:1], group_size) == account_id
-                column = jnp.transpose(fields)[:, 1:2]
-                bound = jnp.broadcast_to(column, (cells, bins)).astype(jnp.bfloat16)
-                right = jnp.where(bin_id >= bound, rowed(ratio[pl.ds(t, 1), :], cells), zero)
-                for h in range(groups):
-                    part = jnp.where(fields[3:4] == h, rest, 0.0)
-                    left = jnp.where(hit, rowed(part, group_size), zero)
-                    total[pl.ds(h * group_size, group_size), :] += jnp.dot(
-                        left, right, preferred_element_type=jnp.float32
-                    )
-
-            return 0
-
-        lax.fori_loop(0, tiles, dense, 0)
+        tile_id = lax.broadcasted_iota(jnp.int32, (tiles, cells), 0).astype(jnp.float32)
+
+        def dense(left_over):
+            t = left_over.astype(jnp.int32)
+            place = places[pl.ds(t, 1), :]
+            rest = jnp.where(place < 0, value_all[pl.ds(t, 1), :], 0.0)
+            hit = rowed(low_all[pl.ds(t, 1), :], group_size) == account_id
+            column = jnp.transpose(spread(bound_all, t)).astype(jnp.bfloat16)[:, 0:1]
+            right = jnp.where(
+                bin_id >= jnp.broadcast_to(column, (cells, bins)),
+                rowed(ratio[pl.ds(t, 1), :], cells),
+                zero,
+            )
+            for h in range(groups):
+                part = jnp.where(place == -1.0 - h, rest, 0.0)
+                left = jnp.where(hit, rowed(part, group_size), zero)
+                total[pl.ds(h * group_size, group_size), :] += jnp.dot(
+                    left, right, preferred_element_type=jnp.float32
+                )
+            return jnp.max(jnp.where((places[...] < 0) & (tile_id < left_over), tile_id, -1.0))
+
+        lax.while_loop(
+            lambda t: t >= 0, dense, jnp.max(jnp.where(places[...] < 0, tile_id, -1.0))
+        )
 
 
 def losses(low, bound, value, ratio, account_count):
@@ -533,22 +544,20 @@
     groups = GROUPS
     together = groups // 2
     gathered = pltpu.VMEM((groups, tiles // together, cells), jnp.float32)
+    whole = pltpu.VMEM((tiles, cells), jnp.float32)
     return pl.pallas_call(
         loss_kernel,
         out_shape=jax.ShapeDtypeStruct((account_count, bins), jnp.float32),
         in_specs=[VMEM] * 4,
         out_specs=VMEM,
-        scratch_shapes=[
-            pltpu.VMEM((tiles, bins), jnp.float32),
-            pltpu.VMEM((tiles, 8, cells), jnp.float32),
-            pltpu.VMEM((tiles, cells), jnp.float32),
-            gathered, gathered, gathered,
+        scratch_shapes=[pltpu.VMEM((tiles, bins), jnp.float32)]
+        + [whole] * 4
+        + [gathered] * 3
+        + [
+            pltpu.VMEM((account_count // groups, SPAN * cells), jnp.bfloat16),
+            pltpu.VMEM((SPAN * cells, bins), jnp.bfloat16),
         ]
-        + [
-            pltpu.VMEM((account_count // groups, CHUNK // HALVES * cells), jnp.bfloat16),
-            pltpu.VMEM((CHUNK // HALVES * cells, bins), jnp.bfloat16),
-        ]
-        * HALVES,
+        * BUFFERS,
         name="losses",
     )(low, bound, value, ratio)
 

time: 104 us -> 72.3 us (0.70)
  Pallas kernels: 99.7 us -> 68.2 us
    pallas_call x1, Pallas kernels: 54.6 us -> 23 us  [losses(): pl.pallas_call(loss_kernel, out_shape=jax.ShapeDtypeStruct((account_count...]
where the time goes in v2:
time: 72.3 us; the launch traced here: 72.1 us
  Pallas kernels  68.2 us (94%)
  local copies, waits for them, and re-layouts  3.22 us (4%)
    pallas_call x1, Pallas kernels, losses(): pl.pallas_call(loss_kernel, out_shape=jax.ShapeDtypeStruct((account_count...  23 us
    pallas_call x1, Pallas kernels, exchange(): pl.pallas_call(functools.partial(exchange_kernel, jobs), out_shape=shapes...  16.6 us
    pallas_call x1, Pallas kernels, settle(): pl.pallas_call(functools.partial(settle_kernel, scale), out_shape=(jax.Sh...  15.7 us
    pallas_call x1, Pallas kernels, front(): pl.pallas_call(front_kernel, out_shape=(jax.ShapeDtypeStruct((rows, width...  12.8 us
    unnamed x7, local copies, waits for them, and re-layouts  3.22 us

profile of v2, /device:TPU:0, one launch (start us, length us, event | category | flops | bytes accessed | tf_op | source)
XLA Modules:
  0.0 72.1 jit_solution(2600292184837961319)
XLA Ops:
  0.6 12.8 %front.1 = (f32[32,1024]{1,0:T(8,128)}, bf16[256,256]{1,0:T(8,128)(2,1)}, bf16[256,128]{1,0:T(8,128)(2,1)}, bf16[256,128]{1,0:T(8,128)(2,1)}, bf16[256,128]{1,0:T(8,128)(2,1)}) custom-call(f32[32,1024]{1,0:T(8,128)} %bitcast.14, f32[32,1024]{1,0:T(8,128)} %bed_here.1, s32[32,1024]{1,0:T(8,128)} %bitcast.15, s32[384,128]{1,0:T(8,128)} %account.1, ...), custom_call_target="tpu_custom_call" | custom-call | tf_op jit(solution)/shard_map/front/pallas_call | solution.py:357
  13.5 23.0 %losses.1 = f32[1024,256]{1,0:T(8,128)} custom-call(bf16[256,128]{1,0:T(8,128)(2,1)} %get-tuple-element.11.low_in, bf16[256,128]{1,0:T(8,128)(2,1)} %get-tuple-element.12.bin_in, bf16[256,128]{1,0:T(8,128)(2,1)} %get-tuple-element.13.value_in, bf16[256,256]{1,0:T(8,128)(2,1)} %get-tuple-element.14.ratio_in), custom_call_target="tpu_custom_call" | custom-call | tf_op jit(solution)/shard_map/losses/pallas_call | solution.py:548
  36.5 16.6 %exchange2.1.parts = f32[8,128,256]{2,1,0:T(8,128)} custom-call(f32[8,128,256]{2,1,0:T(8,128)} %bitcast.10), custom_call_target="tpu_custom_call" | custom-call | tf_op jit(solution)/shard_map/exchange2/pallas_call | solution.py:75
  53.1 0.0 copy-start
  53.1 15.7 %settle.1 = (bf16[8,128,256]{2,1,0:T(8,128)(2,1)}, f32[4,32,256]{2,1,0:T(8,128)}) custom-call(f32[8,128,256]{2,1,0:T(8,128)} %exchange2.1.parts, f32[1,1024]{1,0:T(1,128)} %bitcast.16, f32[1,1024]{1,0:T(1,128)} %bitcast.17), custom_call_target="tpu_custom_call" | custom-call | tf_op jit(solution)/shard_map/settle/pallas_call | solution.py:166
  68.9 0.0 copy-done
  68.9 0.7 copy.17
  69.5 0.0 copy-start.1
  69.5 1.9 %copy.18 = bf16[1,1024,256]{2,1,0:T(8,128)(2,1)} copy(bf16[1,1024,256]{2,1,0:T(8,128)(2,1)} %bitcast.11) | data formatting | bytes 1048576
  71.4 0.0 copy-done.1
  71.4 0.7 copy.19
Async XLA Ops:
  53.1 15.7 %copy-start = (f32[32,1024]{1,0:T(8,128)S(1)}, f32[32,1024]{1,0:T(8,128)}, u32[]{:S(2)}) copy-start(f32[32,1024]{1,0:T(8,128)} %get-tuple-element.10) | copy-start | bytes 393220
  69.5 1.9 %copy-start.1 = (f32[4,32,256]{2,1,0:T(8,128)S(1)}, f32[4,32,256]{2,1,0:T(8,128)}, u32[]{:S(2)}) copy-start(f32[4,32,256]{2,1,0:T(8,128)} %get-tuple-element.16) | copy-start | bytes 393220

commit v3 on v2

--- a/solution.py
+++ b/solution.py
@@ -11,8 +11,7 @@
 CHUNK = 8
 GROUPS = 8
 SPAN = 32
-BUFFERS = 2
-UNROLL = 8
+UNROLL = 16
 
 courant = 0.5
 gravity = 1.0
@@ -388,7 +387,7 @@
 
 def loss_kernel(
     low_in, bin_in, value_in, ratio_in, total,
-    ratio, low_all, bound_all, value_all, places, lows, bounds, values, *halves,
+    ratio_all, ratio, low_all, bound_all, value_all, places, lows, bounds, values,
 ):
     accounts, bins = total.shape
     tiles, cells = low_in.shape
@@ -407,8 +406,8 @@
     group = low.astype(jnp.int32) // group_size
     low_all[...] = low - (group * group_size).astype(jnp.float32)
     bound_all[...] = jnp.where(bound < 0, bound + 256.0, bound)
+    ratio_all[...] = ratio_in[...].astype(jnp.float32)
     value_all[...] = value_in[...].astype(jnp.float32)
-    ratio[...] = ratio_in[...].astype(jnp.float32)
     earlier = jnp.where(
         lax.broadcasted_iota(jnp.int32, (cells, cells), 0)
         < lax.broadcasted_iota(jnp.int32, (cells, cells), 1),
@@ -440,6 +439,11 @@
     def gather(number, _):
         for u in range(unroll):
             bundle = number * unroll + u
+            for j in range(together):
+                t = bundle * together + j
+                ratio[bundle, j] = jnp.broadcast_to(
+                    ratio_all[pl.ds(t, 1), :], (16, bins)
+                ).astype(jnp.bfloat16)
             found = []
             for j in range(together):
                 t = bundle * together + j
@@ -473,35 +477,39 @@
 
     account_id = numbered(group_size, cells, 0)
     bin_id = jnp.concatenate([numbered(16, bins, 1)] * (cells // 16), axis=0)
-    buffers = len(halves) // 2
-    span = halves[1].shape[0] // cells
+    span = min(SPAN, bundles)
 
     def one_group(h, _):
         rows = pl.ds(pl.multiple_of(h * group_size, group_size), group_size)
+        turned = [lax.rem(e + groups - h, together) for e in range(together)]
         summed = None
         for c in range(bundles // span):
-            left, right = halves[c % buffers * 2 : c % buffers * 2 + 2]
+            left, right = [], []
             for block in range(span // CHUNK):
                 first = c * span + block * CHUNK
                 columns = jnp.transpose(bounds[h, first : first + CHUNK, :]).astype(jnp.bfloat16)
                 for i in range(CHUNK):
                     bundle = first + i
-                    spot = slice((block * CHUNK + i) * cells, (block * CHUNK + i + 1) * cells)
-                    left[:, spot] = jnp.where(
-                        rowed(lows[h, bundle : bundle + 1, :], group_size) == account_id,
-                        rowed(values[h, bundle : bundle + 1, :], group_size),
-                        zero,
+                    left.append(
+                        jnp.where(
+                            rowed(lows[h, bundle : bundle + 1, :], group_size) == account_id,
+                            rowed(values[h, bundle : bundle + 1, :], group_size),
+                            zero,
+                        )
                     )
                     shown = []
                     for e in range(together):
-                        t = bundle * together + lax.rem(e + groups - h, together)
-                        shown.append(rowed(ratio[pl.ds(t, 1), :], capacity))
-                    right[spot, :] = jnp.where(
-                        bin_id >= jnp.broadcast_to(columns[:, i : i + 1], (cells, bins)),
-                        jnp.concatenate(shown, axis=0),
-                        zero,
+                        row = ratio[bundle, turned[e]]
+                        shown.extend([row] * (capacity // 16))
+                    bound = jnp.broadcast_to(columns[:, i : i + 1], (cells, bins))
+                    right.append(
+                        jnp.where(bin_id >= bound, jnp.concatenate(shown, axis=0), zero)
                     )
-            part = jnp.dot(left[...], right[...], preferred_element_type=jnp.float32)
+            part = jnp.dot(
+                jnp.concatenate(left, axis=1),
+                jnp.concatenate(right, axis=0),
+                preferred_element_type=jnp.float32,
+            )
             summed = part if summed is None else summed + part
         total[rows, :] = summed
         return 0
@@ -522,7 +530,7 @@
             column = jnp.transpose(spread(bound_all, t)).astype(jnp.bfloat16)[:, 0:1]
             right = jnp.where(
                 bin_id >= jnp.broadcast_to(column, (cells, bins)),
-                rowed(ratio[pl.ds(t, 1), :], cells),
+                rowed(ratio_all[pl.ds(t, 1), :], cells),
                 zero,
             )
             for h in range(groups):
@@ -550,14 +558,12 @@
         out_shape=jax.ShapeDtypeStruct((account_count, bins), jnp.float32),
         in_specs=[VMEM] * 4,
         out_specs=VMEM,
-        scratch_shapes=[pltpu.VMEM((tiles, bins), jnp.float32)]
+        scratch_shapes=[
+            pltpu.VMEM((tiles, bins), jnp.float32),
+            pltpu.VMEM((tiles // together, together, 16, bins), jnp.bfloat16),
+        ]
         + [whole] * 4
-        + [gathered] * 3
-        + [
-            pltpu.VMEM((account_count // groups, SPAN * cells), jnp.bfloat16),
-            pltpu.VMEM((SPAN * cells, bins), jnp.bfloat16),
-        ]
-        * BUFFERS,
+        + [gathered] * 3,
         name="losses",
     )(low, bound, value, ratio)
 

time: 72.3 us -> 69.7 us (0.964)
  Pallas kernels: 68.2 us -> 65.6 us
    pallas_call x1, Pallas kernels: 23 us -> 20.4 us  [losses(): pl.pallas_call(loss_kernel, out_shape=jax.ShapeDtypeStruct((account_count...]
where the time goes in v3:
time: 69.7 us; the launch traced here: 69.5 us
  Pallas kernels  65.6 us (94%)
  local copies, waits for them, and re-layouts  3.22 us (5%)
    pallas_call x1, Pallas kernels, losses(): pl.pallas_call(loss_kernel, out_shape=jax.ShapeDtypeStruct((account_count...  20.4 us
    pallas_call x1, Pallas kernels, exchange(): pl.pallas_call(functools.partial(exchange_kernel, jobs), out_shape=shapes...  16.6 us
    pallas_call x1, Pallas kernels, settle(): pl.pallas_call(functools.partial(settle_kernel, scale), out_shape=(jax.Sh...  15.7 us
    pallas_call x1, Pallas kernels, front(): pl.pallas_call(front_kernel, out_shape=(jax.ShapeDtypeStruct((rows, width...  12.8 us
    unnamed x7, local copies, waits for them, and re-layouts  3.22 us

profile of v3, /device:TPU:0, one launch (start us, length us, event | category | flops | bytes accessed | tf_op | source)
XLA Modules:
  0.0 69.5 jit_solution(12165574376615168123)
XLA Ops:
  0.6 12.8 %front.1 = (f32[32,1024]{1,0:T(8,128)}, bf16[256,256]{1,0:T(8,128)(2,1)}, bf16[256,128]{1,0:T(8,128)(2,1)}, bf16[256,128]{1,0:T(8,128)(2,1)}, bf16[256,128]{1,0:T(8,128)(2,1)}) custom-call(f32[32,1024]{1,0:T(8,128)} %bitcast.14, f32[32,1024]{1,0:T(8,128)} %bed_here.1, s32[32,1024]{1,0:T(8,128)} %bitcast.15, s32[384,128]{1,0:T(8,128)} %account.1, ...), custom_call_target="tpu_custom_call" | custom-call | tf_op jit(solution)/shard_map/front/pallas_call | solution.py:356
  13.5 20.4 %losses.1 = f32[1024,256]{1,0:T(8,128)} custom-call(bf16[256,128]{1,0:T(8,128)(2,1)} %get-tuple-element.11.low_in, bf16[256,128]{1,0:T(8,128)(2,1)} %get-tuple-element.12.bin_in, bf16[256,128]{1,0:T(8,128)(2,1)} %get-tuple-element.13.value_in, bf16[256,256]{1,0:T(8,128)(2,1)} %get-tuple-element.14.ratio_in), custom_call_target="tpu_custom_call" | custom-call | tf_op jit(solution)/shard_map/losses/pallas_call | solution.py:556
  33.9 16.6 %exchange2.1.parts = f32[8,128,256]{2,1,0:T(8,128)} custom-call(f32[8,128,256]{2,1,0:T(8,128)} %bitcast.10), custom_call_target="tpu_custom_call" | custom-call | tf_op jit(solution)/shard_map/exchange2/pallas_call | solution.py:74
  50.5 0.0 copy-start
  50.5 15.7 %settle.1 = (bf16[8,128,256]{2,1,0:T(8,128)(2,1)}, f32[4,32,256]{2,1,0:T(8,128)}) custom-call(f32[8,128,256]{2,1,0:T(8,128)} %exchange2.1.parts, f32[1,1024]{1,0:T(1,128)} %bitcast.16, f32[1,1024]{1,0:T(1,128)} %bitcast.17), custom_call_target="tpu_custom_call" | custom-call | tf_op jit(solution)/shard_map/settle/pallas_call | solution.py:165
  66.3 0.0 copy-done
  66.3 0.7 copy.17
  66.9 0.0 copy-start.1
  66.9 1.9 %copy.18 = bf16[1,1024,256]{2,1,0:T(8,128)(2,1)} copy(bf16[1,1024,256]{2,1,0:T(8,128)(2,1)} %bitcast.11) | data formatting | bytes 1048576
  68.8 0.0 copy-done.1
  68.8 0.7 copy.19
Async XLA Ops:
  50.5 15.7 %copy-start = (f32[32,1024]{1,0:T(8,128)S(1)}, f32[32,1024]{1,0:T(8,128)}, u32[]{:S(2)}) copy-start(f32[32,1024]{1,0:T(8,128)} %get-tuple-element.10) | copy-start | bytes 393220
  66.9 1.9 %copy-start.1 = (f32[4,32,256]{2,1,0:T(8,128)S(1)}, f32[4,32,256]{2,1,0:T(8,128)}, u32[]{:S(2)}) copy-start(f32[4,32,256]{2,1,0:T(8,128)} %get-tuple-element.16) | copy-start | bytes 393220

commit v4 on v3

--- a/solution.py
+++ b/solution.py
@@ -77,7 +77,7 @@
         in_specs=[VMEM] * len(arrays),
         out_specs=[VMEM] * len(arrays),
         scratch_shapes=scratch,
-        compiler_params=pltpu.CompilerParams(collective_id=number, has_side_effects=True),
+        compiler_params=pltpu.CompilerParams(collective_id=number, has_side_effects=True, vmem_limit_bytes=16*2**20),
         name="exchange" + str(number),
     )(*arrays)
 
@@ -182,7 +182,7 @@
         ]
         + [dma((owners,))] * 2
         + [dma((events,))] * 4,
-        compiler_params=pltpu.CompilerParams(collective_id=number, has_side_effects=True),
+        compiler_params=pltpu.CompilerParams(collective_id=number, has_side_effects=True, vmem_limit_bytes=16*2**20),
         name="settle",
     )(parts, floor, roof)
 
@@ -367,7 +367,7 @@
         + [dma((6,))] * 2
         + [dma((size,))] * 2
         + [dma((2,))],
-        compiler_params=pltpu.CompilerParams(collective_id=number, has_side_effects=True),
+        compiler_params=pltpu.CompilerParams(collective_id=number, has_side_effects=True, vmem_limit_bytes=16*2**20),
         name="front",
     )(*strips, *records, owner_row, weight, bias)
 
@@ -564,7 +564,7 @@
         ]
         + [whole] * 4
         + [gathered] * 3,
-        name="losses",
+        compiler_params=pltpu.CompilerParams(vmem_limit_bytes=24*2**20), name="losses",
     )(low, bound, value, ratio)
 
 

time: 69.7 us -> 67.6 us (0.970)
  Pallas kernels: 65.6 us -> 57.5 us
  local copies, waits for them, and re-layouts: 3.22 us -> 9.09 us
    unnamed x7 -> x25, local copies, waits for them, and re-layouts: 3.22 us -> 9.09 us
    pallas_call x1, Pallas kernels: 16.6 us -> 14.4 us  [exchange(): pl.pallas_call(functools.partial(exchange_kernel, jobs), out_shape=shapes...]
    pallas_call x1, Pallas kernels: 15.7 us -> 13.7 us  [settle(): pl.pallas_call(functools.partial(settle_kernel, scale), out_shape=(jax.Sh...]
    pallas_call x1, Pallas kernels: 20.4 us -> 18.5 us  [losses(): pl.pallas_call(loss_kernel, out_shape=jax.ShapeDtypeStruct((account_count...]
    pallas_call x1, Pallas kernels: 12.8 us -> 10.9 us  [front(): pl.pallas_call(front_kernel, out_shape=(jax.ShapeDtypeStruct((rows, width...]
where the time goes in v4:
time: 67.6 us; the launch traced here: 67.3 us
  Pallas kernels  57.5 us (85%)
  local copies, waits for them, and re-layouts  9.09 us (13%)
  between operations  0.72 us (1%)
    pallas_call x1, Pallas kernels, losses(): pl.pallas_call(loss_kernel, out_shape=jax.ShapeDtypeStruct((account_count...  18.5 us
    pallas_call x1, Pallas kernels, exchange(): pl.pallas_call(functools.partial(exchange_kernel, jobs), out_shape=shapes...  14.4 us
    pallas_call x1, Pallas kernels, settle(): pl.pallas_call(functools.partial(settle_kernel, scale), out_shape=(jax.Sh...  13.7 us
    pallas_call x1, Pallas kernels, front(): pl.pallas_call(front_kernel, out_shape=(jax.ShapeDtypeStruct((rows, width...  10.9 us
    unnamed x25, local copies, waits for them, and re-layouts  9.09 us

profile of v4, /device:TPU:0, one launch (start us, length us, event | category | flops | bytes accessed | tf_op | source)
XLA Modules:
  0.0 67.3 jit_solution(13466020987592578400)
XLA Ops:
  0.6 0.0 copy-start.10
  0.6 0.0 copy-start.9
  0.7 0.7 copy-done.10
  1.3 0.0 copy-done.9
  1.3 0.9 %copy-done = s32[384,128]{1,0:T(8,128)S(1)} copy-done((s32[384,128]{1,0:T(8,128)S(1)}, s32[384,128]{1,0:T(8,128)}, u32[]{:S(2)}) %copy-start) | copy-done | bytes 196632
  2.3 0.0 copy-start.1
  2.3 0.9 %copy-done.1 = s32[384,128]{1,0:T(8,128)S(1)} copy-done((s32[384,128]{1,0:T(8,128)S(1)}, s32[384,128]{1,0:T(8,128)}, u32[]{:S(2)}) %copy-start.1) | copy-done | bytes 196632
  3.2 0.0 copy-start.2
  3.2 0.9 %copy-done.2 = f32[1,32,1024]{2,1,0:T(8,128)S(1)} copy-done((f32[1,32,1024]{2,1,0:T(8,128)S(1)}, f32[1,32,1024]{2,1,0:T(8,128)}, u32[]{:S(2)}) %copy-start.2) | copy-done | bytes 131096
  4.1 0.9 %copy-done.3 = f32[32,1024]{1,0:T(8,128)S(1)} copy-done((f32[32,1024]{1,0:T(8,128)S(1)}, f32[32,1024]{1,0:T(8,128)}, u32[]{:S(2)}) %copy-start.3) | copy-done | bytes 131096
  5.0 0.9 %copy-done.4 = s32[1,32,1024]{2,1,0:T(8,128)S(1)} copy-done((s32[1,32,1024]{2,1,0:T(8,128)S(1)}, s32[1,32,1024]{2,1,0:T(8,128)}, u32[]{:S(2)}) %copy-start.4) | copy-done | bytes 131096
  5.9 0.9 %copy-done.5 = bf16[384,128]{1,0:T(8,128)(2,1)S(1)} copy-done((bf16[384,128]{1,0:T(8,128)(2,1)S(1)}, bf16[384,128]{1,0:T(8,128)(2,1)}, u32[]{:S(2)}) %copy-start.5) | copy-done | bytes 98328
  6.8 0.8 %copy-done.6 = bf16[128,256]{1,0:T(8,128)(2,1)S(1)} copy-done((bf16[128,256]{1,0:T(8,128)(2,1)S(1)}, bf16[128,256]{1,0:T(8,128)(2,1)}, u32[]{:S(2)}) %copy-start.6) | copy-done | bytes 65560
  7.6 10.9 %front.1 = (f32[32,1024]{1,0:T(8,128)S(1)}, bf16[256,256]{1,0:T(8,128)(2,1)S(1)}, bf16[256,128]{1,0:T(8,128)(2,1)S(1)}, bf16[256,128]{1,0:T(8,128)(2,1)S(1)}, bf16[256,128]{1,0:T(8,128)(2,1)S(1)}) custom-call(f32[32,1024]{1,0:T(8,128)S(1)} %bitcast.14, f32[32,1024]{1,0:T(8,128)S(1)} %copy-done.3, s32[32,1024]{1,0:T(8,128)S(1)} %bitcast.15, ...), custom_call_target="tpu_custom_call" | custom-call | tf_op jit(solution)/shard_map/front/pallas_call | solution.py:356
  18.6 18.5 %losses.1 = f32[1024,256]{1,0:T(8,128)S(1)} custom-call(bf16[256,128]{1,0:T(8,128)(2,1)S(1)} %get-tuple-element.11.low_in, bf16[256,128]{1,0:T(8,128)(2,1)S(1)} %get-tuple-element.12.bin_in, bf16[256,128]{1,0:T(8,128)(2,1)S(1)} %get-tuple-element.13.value_in, bf16[256,256]{1,0:T(8,128)(2,1)S(1)} %get-tuple-element.14.ratio_in), custom_call_target="tpu_custom_call" | custom-call | tf_op jit(solution)/shard_map/losses/pallas_call | solution.py:556
  37.0 0.0 copy-start.7
  37.0 0.0 copy-start.8
  37.1 14.4 %exchange2.1.parts = f32[8,128,256]{2,1,0:T(8,128)S(1)} custom-call(f32[8,128,256]{2,1,0:T(8,128)S(1)} %bitcast.10), custom_call_target="tpu_custom_call" | custom-call | tf_op jit(solution)/shard_map/exchange2/pallas_call | solution.py:74
  51.4 0.0 copy-done.7
  51.4 0.0 copy-done.8
  51.4 13.7 %settle.1 = (bf16[8,128,256]{2,1,0:T(8,128)(2,1)S(1)}, f32[4,32,256]{2,1,0:T(8,128)S(1)}) custom-call(f32[8,128,256]{2,1,0:T(8,128)S(1)} %exchange2.1.parts, f32[1,1024]{1,0:T(1,128)S(1)} %bitcast.16, f32[1,1024]{1,0:T(1,128)S(1)} %bitcast.17), custom_call_target="tpu_custom_call" | custom-call | tf_op jit(solution)/shard_map/settle/pallas_call | solution.py:165
  65.2 0.7 copy.17
  65.8 0.8 %copy.18 = bf16[1,1024,256]{2,1,0:T(8,128)(2,1)} copy(bf16[1,1024,256]{2,1,0:T(8,128)(2,1)S(1)} %bitcast.11) | data formatting | bytes 1048576
  66.6 0.7 copy.19
  (5 shorter events, 0.0 us)
Async XLA Ops:
  0.6 0.7 %copy-start.10 = (f32[256]{0:T(256)S(1)}, f32[256]{0:T(256)}, u32[]{:S(2)}) copy-start(f32[256]{0:T(256)} %param.16) | copy-start | bytes 3076
  0.6 0.7 %copy-start.9 = (s32[256,1]{0,1:T(1,128)S(1)}, s32[256,1]{0,1:T(1,128)}, u32[]{:S(2)}) copy-start(s32[256,1]{0,1:T(1,128)} %param.14) | copy-start | bytes 3076
  1.3 0.9 %copy-start = (s32[384,128]{1,0:T(8,128)S(1)}, s32[384,128]{1,0:T(8,128)}, u32[]{:S(2)}) copy-start(s32[384,128]{1,0:T(8,128)} %account.1) | copy-start | bytes 589828
  2.3 0.9 %copy-start.1 = (s32[384,128]{1,0:T(8,128)S(1)}, s32[384,128]{1,0:T(8,128)}, u32[]{:S(2)}) copy-start(s32[384,128]{1,0:T(8,128)} %threshold.1) | copy-start | bytes 589828
  3.2 0.9 %copy-start.2 = (f32[1,32,1024]{2,1,0:T(8,128)S(1)}, f32[1,32,1024]{2,1,0:T(8,128)}, u32[]{:S(2)}) copy-start(f32[1,32,1024]{2,1,0:T(8,128)} %param.11) | copy-start | bytes 393220
  4.1 0.9 %copy-start.3 = (f32[32,1024]{1,0:T(8,128)S(1)}, f32[32,1024]{1,0:T(8,128)}, u32[]{:S(2)}) copy-start(f32[32,1024]{1,0:T(8,128)} %bed_here.1) | copy-start | bytes 393220
  5.0 0.9 %copy-start.4 = (s32[1,32,1024]{2,1,0:T(8,128)S(1)}, s32[1,32,1024]{2,1,0:T(8,128)}, u32[]{:S(2)}) copy-start(s32[1,32,1024]{2,1,0:T(8,128)} %param.13) | copy-start | bytes 393220
  5.9 0.9 %copy-start.5 = (bf16[384,128]{1,0:T(8,128)(2,1)S(1)}, bf16[384,128]{1,0:T(8,128)(2,1)}, u32[]{:S(2)}) copy-start(bf16[384,128]{1,0:T(8,128)(2,1)} %value.1) | copy-start | bytes 294916
  6.8 0.8 %copy-start.6 = (bf16[128,256]{1,0:T(8,128)(2,1)S(1)}, bf16[128,256]{1,0:T(8,128)(2,1)}, u32[]{:S(2)}) copy-start(bf16[128,256]{1,0:T(8,128)(2,1)} %weight.1) | copy-start | bytes 196612
  37.0 14.4 %copy-start.7 = (f32[1024]{0:T(1024)S(1)}, f32[1024]{0:T(1024)}, u32[]{:S(2)}) copy-start(f32[1024]{0:T(1024)} %param.20) | copy-start | bytes 12292
  37.0 14.4 %copy-start.8 = (f32[1024]{0:T(1024)S(1)}, f32[1024]{0:T(1024)}, u32[]{:S(2)}) copy-start(f32[1024]{0:T(1024)} %param.21) | copy-start | bytes 12292

commit v5 on v4

--- a/solution.py
+++ b/solution.py
@@ -9,6 +9,7 @@
 
 SUBSTEPS = 8
 CHUNK = 8
+LIMIT = 24 * 2**20
 GROUPS = 8
 SPAN = 32
 UNROLL = 16
@@ -17,174 +18,12 @@
 gravity = 1.0
 
 VMEM = pl.BlockSpec(memory_space=pltpu.VMEM)
-SMEM = pl.BlockSpec(memory_space=pltpu.SMEM)
+HBM = pl.BlockSpec(memory_space=pltpu.HBM)
 MESH = pl.DeviceIdType.MESH
 
 
-def exchange_kernel(jobs, *refs):
-    count = len(jobs)
-    sources, targets, sems = refs[:count], refs[count : 2 * count], refs[2 * count :]
-    barrier = pltpu.get_barrier_semaphore()
-    greeted = 0
-    for axis in dict.fromkeys(axis for axis, _ in jobs):
-        size = lax.axis_size(axis)
-        me = lax.axis_index(axis)
-        for hop in range(1, size):
-            pl.semaphore_signal(
-                barrier, inc=1, device_id={axis: lax.rem(me + hop, size)}, device_id_type=MESH
-            )
-        greeted += size - 1
-    pl.semaphore_wait(barrier, greeted)
-    copies = []
-    for job, (axis, spread) in enumerate(jobs):
-        source, target = sources[job], targets[job]
-        local, sent, received = sems[3 * job : 3 * job + 3]
-        size = lax.axis_size(axis)
-        me = lax.axis_index(axis)
-        for hop in range(1, size):
-            peer = lax.rem(me + hop, size)
-            copy = pltpu.make_async_remote_copy(
-                src_ref=source if spread else source.at[peer],
-                dst_ref=target.at[me],
-                send_sem=sent.at[hop],
-                recv_sem=received.at[hop],
-                device_id={axis: peer},
-                device_id_type=MESH,
-            )
-            copy.start()
-            copies.append(copy)
-        own = pltpu.make_async_copy(source if spread else source.at[me], target.at[me], local)
-        own.start()
-        copies.append(own)
-    for copy in copies:
-        copy.wait()
-
-
-def exchange(arrays, jobs, number):
-    shapes, scratch = [], []
-    for array, (axis, spread) in zip(arrays, jobs):
-        size = lax.axis_size(axis)
-        shape = (size,) + array.shape if spread else array.shape
-        shapes.append(jax.ShapeDtypeStruct(shape, array.dtype))
-        scratch += [
-            pltpu.SemaphoreType.DMA,
-            pltpu.SemaphoreType.DMA((size,)),
-            pltpu.SemaphoreType.DMA((size,)),
-        ]
-    return pl.pallas_call(
-        functools.partial(exchange_kernel, jobs),
-        out_shape=shapes,
-        in_specs=[VMEM] * len(arrays),
-        out_specs=[VMEM] * len(arrays),
-        scratch_shapes=scratch,
-        compiler_params=pltpu.CompilerParams(collective_id=number, has_side_effects=True, vmem_limit_bytes=16*2**20),
-        name="exchange" + str(number),
-    )(*arrays)
-
-
-def settle_kernel(
-    scale, parts, floor, roof, net_loss, portfolio,
-    made, made_low, kept, kept_low, arrived, summed, kept_sum, local,
-    sent_low, got_low, sent_net, got_net, sent_sum, got_sum,
-):
-    owners, share_rows, _ = parts.shape
-    events = lax.axis_size("event")
-    me, group = lax.axis_index("terrain"), lax.axis_index("event")
-    barrier = pltpu.get_barrier_semaphore()
-    for axis, size, mine in (("terrain", owners, me), ("event", events, group)):
-        for hop in range(1, size):
-            pl.semaphore_signal(
-                barrier, inc=1, device_id={axis: lax.rem(mine + hop, size)}, device_id_type=MESH
-            )
-    whole = parts[0]
-    for n in range(1, owners):
-        whole = whole + parts[n]
-    picked = (share_rows, floor.shape[1])
-    account = lax.broadcasted_iota(jnp.int32, picked, 1)
-    mine = account == lax.broadcasted_iota(jnp.int32, picked, 0) + me * share_rows
-
-    def of_share(terms):
-        return jnp.sum(jnp.where(mine, terms[...], 0.0), axis=1, keepdims=True)
-
-    net = jnp.minimum(jnp.maximum(whole * scale - of_share(floor), 0.0), of_share(roof))
-    made[...] = net.reshape(made.shape)
-    made_low[...] = net.astype(made_low.dtype)
-    first = [
-        pltpu.make_async_copy(made, kept, local.at[0]),
-        pltpu.make_async_copy(made_low, kept_low, local.at[1]),
-    ]
-    for copy in first:
-        copy.start()
-    pl.semaphore_wait(barrier, owners + events - 2)
-    for copy in first:
-        copy.wait()
-
-    def push(axis, size, index, source, target, sent, received, split):
-        copies = []
-        for hop in range(1, size):
-            peer = lax.rem(index + hop, size)
-            copy = pltpu.make_async_remote_copy(
-                src_ref=source.at[peer] if split else source,
-                dst_ref=target.at[index],
-                send_sem=sent.at[hop],
-                recv_sem=received.at[hop],
-                device_id={axis: peer},
-                device_id_type=MESH,
-            )
-            copy.start()
-            copies.append(copy)
-        return copies
-
-    nets = push("event", events, group, kept, arrived, sent_net, got_net, True)
-    own_net = pltpu.make_async_copy(kept.at[group], arrived.at[group], local.at[2])
-    own_net.start()
-    lows = push("terrain", owners, me, kept_low, net_loss, sent_low, got_low, False)
-    own_low = pltpu.make_async_copy(kept_low, net_loss.at[me], local.at[3])
-    own_low.start()
-    for copy in nets + [own_net]:
-        copy.wait()
-    total = arrived[0]
-    for n in range(1, events):
-        total = total + arrived[n]
-    summed[...] = total / events
-    last = pltpu.make_async_copy(summed, kept_sum, local.at[4])
-    last.start()
-    last.wait()
-    sums = push("event", events, group, kept_sum, portfolio, sent_sum, got_sum, False)
-    own_sum = pltpu.make_async_copy(kept_sum, portfolio.at[group], local.at[5])
-    own_sum.start()
-    for copy in sums + [own_sum] + lows + [own_low]:
-        copy.wait()
-
-
-def settle(parts, floor, roof, scale, number):
-    owners, share_rows, bins = parts.shape
-    events = lax.axis_size("event")
-    split = (events, share_rows // events, bins)
-    dma = pltpu.SemaphoreType.DMA
-    return pl.pallas_call(
-        functools.partial(settle_kernel, scale),
-        out_shape=(
-            jax.ShapeDtypeStruct((owners, share_rows, bins), jnp.bfloat16),
-            jax.ShapeDtypeStruct(split, jnp.float32),
-        ),
-        in_specs=[VMEM] * 3,
-        out_specs=(VMEM, VMEM),
-        scratch_shapes=[
-            pltpu.VMEM(split, jnp.float32),
-            pltpu.VMEM((share_rows, bins), jnp.bfloat16),
-            pltpu.VMEM(split, jnp.float32),
-            pltpu.VMEM((share_rows, bins), jnp.bfloat16),
-            pltpu.VMEM(split, jnp.float32),
-            pltpu.VMEM(split[1:], jnp.float32),
-            pltpu.VMEM(split[1:], jnp.float32),
-            dma((6,)),
-        ]
-        + [dma((owners,))] * 2
-        + [dma((events,))] * 4,
-        compiler_params=pltpu.CompilerParams(collective_id=number, has_side_effects=True, vmem_limit_bytes=16*2**20),
-        name="settle",
-    )(parts, floor, roof)
+def far(arrays):
+    return [pltpu.with_memory_space_constraint(a, pltpu.HBM) for a in arrays]
 
 
 def padded(count, unit):
@@ -192,8 +31,9 @@
 
 
 def front_kernel(
-    level_here, bed_here, wet_here, account, threshold, value, owner_row, weight, bias,
+    level_far, bed_far, wet_far, account_far, threshold_far, value_far, owner_far, weight_far, bias_far,
     level_out, ratio_out, low_out, bin_out, value_out,
+    level_here, bed_here, wet_here, account, threshold, value, owner_row, weight, bias, loads,
     made, kept, got, level_above, bed_above, wet_above, level_below, bed_below, wet_below,
     halo_sent, halo_got, cell_sent, cell_got, local,
 ):
@@ -204,6 +44,18 @@
         pl.semaphore_signal(
             barrier, inc=1, device_id={"terrain": lax.rem(me + hop, size)}, device_id_type=MESH
         )
+    moved = (
+        (account_far, account), (threshold_far, threshold), (value_far, value),
+        (owner_far, owner_row), (level_far, level_here), (bed_far, bed_here), (wet_far, wet_here),
+        (weight_far, weight), (bias_far, bias),
+    )
+    reads = [
+        pltpu.make_async_copy(far, near, loads.at[n]) for n, (far, near) in enumerate(moved)
+    ]
+    for copy in reads:
+        copy.start()
+    for copy in reads[:4]:
+        copy.wait()
     rows, width = level_here.shape
     capacity = account.shape[0] // size
     room = made.shape[2]
@@ -224,7 +76,7 @@
     pl.semaphore_wait(barrier, size - 1)
 
     later, earlier = lax.rem(me + 1, size), lax.rem(me + size - 1, size)
-    strips = (level_here, bed_here, wet_here)
+    strips = (level_far, bed_far, wet_far)
     above = (level_above, bed_above, wet_above)
     below = (level_below, bed_below, wet_below)
     edges = []
@@ -272,7 +124,7 @@
     slot = lax.broadcasted_iota(jnp.int32, (tiles, size * room), 1).astype(jnp.float32)
     chosen = jnp.where(slot == owner_column * room + rank, 1.0, 0.0).astype(jnp.bfloat16)
 
-    for copy in edges:
+    for copy in reads[4:] + edges:
         copy.wait()
     first_row = me * rows - SUBSTEPS
     total_rows = rows * size
@@ -351,6 +203,7 @@
     tiles = rows * width // cells
     packed = (size, 3, padded(slots // size, 16), cells)
     edge = (SUBSTEPS, width)
+    inputs = strips + records + [owner_row, weight, bias]
     dma = pltpu.SemaphoreType.DMA
     edges = [pltpu.VMEM(edge, f.dtype) for f in strips]
     return pl.pallas_call(
@@ -360,16 +213,20 @@
             jax.ShapeDtypeStruct((tiles, weight.shape[1]), jnp.bfloat16),
         )
         + (jax.ShapeDtypeStruct((tiles, cells), jnp.bfloat16),) * 3,
-        in_specs=[VMEM] * 9,
+        in_specs=[HBM] * 9,
         out_specs=(VMEM,) * 5,
-        scratch_shapes=[pltpu.VMEM(packed, jnp.bfloat16)] * 3
+        scratch_shapes=[pltpu.VMEM(a.shape, a.dtype) for a in inputs]
+        + [dma((9,))]
+        + [pltpu.VMEM(packed, jnp.bfloat16)] * 3
         + edges * 2
         + [dma((6,))] * 2
         + [dma((size,))] * 2
         + [dma((2,))],
-        compiler_params=pltpu.CompilerParams(collective_id=number, has_side_effects=True, vmem_limit_bytes=16*2**20),
+        compiler_params=pltpu.CompilerParams(
+            collective_id=number, has_side_effects=True, vmem_limit_bytes=LIMIT
+        ),
         name="front",
-    )(*strips, *records, owner_row, weight, bias)
+    )(*far(inputs))
 
 
 def rowed(row, height):
@@ -385,10 +242,13 @@
     )
 
 
-def loss_kernel(
-    low_in, bin_in, value_in, ratio_in, total,
-    ratio_all, ratio, low_all, bound_all, value_all, places, lows, bounds, values,
+def sort_kernel(
+    low_in, bin_in, value_in, ratio_in, level_in,
+    lows, bounds, values, ratio, total, level_out,
+    ratio_all, low_all, bound_all, value_all, places,
 ):
+    level_out[...] = level_in[...]
+    total[...] = jnp.zeros(total.shape, jnp.float32)
     accounts, bins = total.shape
     tiles, cells = low_in.shape
     groups = lows.shape[0]
@@ -475,15 +335,122 @@
 
     lax.fori_loop(0, bundles // unroll, gather, 0)
 
+    spilled = jnp.max(rank) >= capacity
+
+    @pl.when(spilled)
+    def _():
+        account_id = numbered(group_size, cells, 0)
+        bin_id = jnp.concatenate([numbered(16, bins, 1)] * (cells // 16), axis=0)
+        tile_id = lax.broadcasted_iota(jnp.int32, (tiles, cells), 0).astype(jnp.float32)
+
+        def dense(left_over):
+            t = left_over.astype(jnp.int32)
+            place = places[pl.ds(t, 1), :]
+            rest = jnp.where(place < 0, value_all[pl.ds(t, 1), :], 0.0)
+            hit = rowed(low_all[pl.ds(t, 1), :], group_size) == account_id
+            column = jnp.transpose(spread(bound_all, t)).astype(jnp.bfloat16)[:, 0:1]
+            right = jnp.where(
+                bin_id >= jnp.broadcast_to(column, (cells, bins)),
+                rowed(ratio_all[pl.ds(t, 1), :], cells),
+                zero,
+            )
+            for h in range(groups):
+                part = jnp.where(place == -1.0 - h, rest, 0.0)
+                left = jnp.where(hit, rowed(part, group_size), zero)
+                total[pl.ds(h * group_size, group_size), :] += jnp.dot(
+                    left, right, preferred_element_type=jnp.float32
+                )
+            return jnp.max(jnp.where((places[...] < 0) & (tile_id < left_over), tile_id, -1.0))
+
+        lax.while_loop(
+            lambda t: t >= 0, dense, jnp.max(jnp.where(places[...] < 0, tile_id, -1.0))
+        )
+
+
+def sort(low, bound, value, ratio, level, account_count):
+    tiles, cells = low.shape
+    bins = ratio.shape[1]
+    together = GROUPS // 2
+    bundles = tiles // together
+    gathered = jax.ShapeDtypeStruct((GROUPS, bundles, cells), jnp.float32)
+    whole = pltpu.VMEM((tiles, cells), jnp.float32)
+    return pl.pallas_call(
+        sort_kernel,
+        out_shape=(
+            gathered,
+            gathered,
+            gathered,
+            jax.ShapeDtypeStruct((bundles, together, 16, bins), jnp.bfloat16),
+            jax.ShapeDtypeStruct((account_count, bins), jnp.float32),
+            jax.ShapeDtypeStruct(level.shape, level.dtype),
+        ),
+        in_specs=[VMEM] * 5,
+        out_specs=(VMEM,) * 6,
+        scratch_shapes=[pltpu.VMEM((tiles, bins), jnp.float32)] + [whole] * 4,
+        compiler_params=pltpu.CompilerParams(vmem_limit_bytes=LIMIT),
+        name="sort",
+    )(low, bound, value, ratio, level)
+
+
+def settle_kernel(
+    scale, lows, bounds, values, ratio, spill, floor_far, roof_far,
+    net_loss, portfolio,
+    floor, roof, total, parts, made, made_low, arrived, summed,
+    sent_part, got_part, sent_low, got_low, sent_more, got_more,
+    sent_net, got_net, sent_sum, got_sum, local,
+):
+    accounts, bins = total.shape
+    owners, share_rows, _ = parts.shape
+    groups, bundles, cells = lows.shape
+    group_size = accounts // groups
+    capacity = 2 * cells // groups
+    together = cells // capacity
+    members = owners // groups
+    zero = jnp.zeros((), jnp.bfloat16)
+    events = lax.axis_size("event")
+    me, group = lax.axis_index("terrain"), lax.axis_index("event")
+    terms = [
+        pltpu.make_async_copy(floor_far, floor, local.at[3]),
+        pltpu.make_async_copy(roof_far, roof, local.at[4]),
+    ]
+    for copy in terms:
+        copy.start()
+    barrier = pltpu.get_barrier_semaphore()
+    for axis, size, mine in (("terrain", owners, me), ("event", events, group)):
+        for hop in range(1, size):
+            pl.semaphore_signal(
+                barrier, inc=1, device_id={axis: lax.rem(mine + hop, size)}, device_id_type=MESH
+            )
+    pl.semaphore_wait(barrier, owners + events - 2)
+
+    def give(owner):
+        hop = lax.rem(owner - me + owners, owners)
+        return pltpu.make_async_remote_copy(
+            src_ref=total.at[pl.ds(pl.multiple_of(owner * share_rows, share_rows), share_rows)],
+            dst_ref=parts.at[me],
+            send_sem=sent_part.at[hop],
+            recv_sem=got_part.at[hop],
+            device_id={"terrain": owner},
+            device_id_type=MESH,
+        )
+
     account_id = numbered(group_size, cells, 0)
     bin_id = jnp.concatenate([numbered(16, bins, 1)] * (cells // 16), axis=0)
     span = min(SPAN, bundles)
 
-    def one_group(h, _):
+    def one_group(number, _):
+        h = lax.rem(me // members + 1 + number, groups)
         rows = pl.ds(pl.multiple_of(h * group_size, group_size), group_size)
         turned = [lax.rem(e + groups - h, together) for e in range(together)]
         summed = None
         for c in range(bundles // span):
+            if c == bundles // span // 2:
+
+                @pl.when(number > 0)
+                def _():
+                    for j in range(members):
+                        give(lax.rem(h + groups - 1, groups) * members + j).start()
+
             left, right = [], []
             for block in range(span // CHUNK):
                 first = c * span + block * CHUNK
@@ -511,61 +478,126 @@
                 preferred_element_type=jnp.float32,
             )
             summed = part if summed is None else summed + part
-        total[rows, :] = summed
+        total[rows, :] = spill[rows, :] + summed
         return 0
 
     lax.fori_loop(0, groups, one_group, 0)
-
-    spilled = jnp.max(rank) >= capacity
-
-    @pl.when(spilled)
-    def _():
-        tile_id = lax.broadcasted_iota(jnp.int32, (tiles, cells), 0).astype(jnp.float32)
-
-        def dense(left_over):
-            t = left_over.astype(jnp.int32)
-            place = places[pl.ds(t, 1), :]
-            rest = jnp.where(place < 0, value_all[pl.ds(t, 1), :], 0.0)
-            hit = rowed(low_all[pl.ds(t, 1), :], group_size) == account_id
-            column = jnp.transpose(spread(bound_all, t)).astype(jnp.bfloat16)[:, 0:1]
-            right = jnp.where(
-                bin_id >= jnp.broadcast_to(column, (cells, bins)),
-                rowed(ratio_all[pl.ds(t, 1), :], cells),
-                zero,
-            )
-            for h in range(groups):
-                part = jnp.where(place == -1.0 - h, rest, 0.0)
-                left = jnp.where(hit, rowed(part, group_size), zero)
-                total[pl.ds(h * group_size, group_size), :] += jnp.dot(
-                    left, right, preferred_element_type=jnp.float32
-                )
-            return jnp.max(jnp.where((places[...] < 0) & (tile_id < left_over), tile_id, -1.0))
-
-        lax.while_loop(
-            lambda t: t >= 0, dense, jnp.max(jnp.where(places[...] < 0, tile_id, -1.0))
-        )
-
-
-def losses(low, bound, value, ratio, account_count):
-    tiles, cells = low.shape
-    bins = ratio.shape[1]
-    groups = GROUPS
-    together = groups // 2
-    gathered = pltpu.VMEM((groups, tiles // together, cells), jnp.float32)
-    whole = pltpu.VMEM((tiles, cells), jnp.float32)
+    for j in range(1, members):
+        give(me // members * members + lax.rem(me + j, members)).start()
+
+    own = pl.ds(pl.multiple_of(me * share_rows, share_rows), share_rows)
+    picked = (share_rows, accounts)
+    account = lax.broadcasted_iota(jnp.int32, picked, 1)
+    mine = account == lax.broadcasted_iota(jnp.int32, picked, 0) + me * share_rows
+
+    def of_share(terms):
+        return jnp.sum(jnp.where(mine, terms[...], 0.0), axis=1, keepdims=True)
+
+    for copy in terms:
+        copy.wait()
+    least, most = of_share(floor), of_share(roof)
+    whole = total[own, :]
+    for hop in range(1, owners):
+        give(lax.rem(me + hop, owners)).wait()
+        whole = whole + parts[lax.rem(me + owners - hop, owners)]
+    net = jnp.minimum(jnp.maximum(whole * scale - least, 0.0), most)
+    made[...] = net.reshape(made.shape)
+    made_low[...] = net.astype(made_low.dtype)
+
+    def push(axis, peer, source, target, sent, received):
+        copy = pltpu.make_async_remote_copy(
+            src_ref=source,
+            dst_ref=target,
+            send_sem=sent,
+            recv_sem=received,
+            device_id={axis: peer},
+            device_id_type=MESH,
+        )
+        copy.start()
+        return copy
+
+    nets, sums = [], []
+    for hop in range(1, events):
+        peer = lax.rem(group + hop, events)
+        nets.append(
+            push("event", peer, made.at[peer], arrived.at[group], sent_net.at[hop], got_net.at[hop])
+        )
+    chips = owners // 2
+    partner = me + 1 - 2 * lax.rem(me, 2)
+    lows_sent = []
+    for k in range(1, chips):
+        peer = lax.rem(me + 2 * k, owners)
+        lows_sent.append(
+            push("terrain", peer, made_low, net_loss.at[me], sent_low.at[k], got_low.at[k])
+        )
+    beside = [
+        push("terrain", partner, made_low, net_loss.at[me], sent_more.at[0], got_more.at[0])
+    ]
+    kept = [
+        pltpu.make_async_copy(made_low, net_loss.at[me], local.at[0]),
+        pltpu.make_async_copy(made.at[group], arrived.at[group], local.at[1]),
+    ]
+    for copy in kept:
+        copy.start()
+    kept[1].wait()
+    for copy in nets:
+        copy.wait()
+    whole = arrived[0]
+    for n in range(1, events):
+        whole = whole + arrived[n]
+    summed[...] = whole / events
+    for hop in range(1, events):
+        peer = lax.rem(group + hop, events)
+        sums.append(
+            push("event", peer, summed, portfolio.at[group], sent_sum.at[hop], got_sum.at[hop])
+        )
+    last = pltpu.make_async_copy(summed, portfolio.at[group], local.at[2])
+    last.start()
+    for k in range(1, chips):
+        lows_sent[k - 1].wait()
+        source = lax.rem(me + owners - 2 * k, owners)
+        beside.append(
+            push(
+                "terrain", partner, net_loss.at[source], net_loss.at[source],
+                sent_more.at[k], got_more.at[k],
+            )
+        )
+    for copy in sums + beside + [kept[0], last]:
+        copy.wait()
+
+
+def settle(lows, bounds, values, ratio, spill, floor, roof, scale, number):
+    account_count, bins = spill.shape
+    owners, events = lax.axis_size("terrain"), lax.axis_size("event")
+    share_rows = account_count // owners
+    split = (events, share_rows // events, bins)
+    dma = pltpu.SemaphoreType.DMA
     return pl.pallas_call(
-        loss_kernel,
-        out_shape=jax.ShapeDtypeStruct((account_count, bins), jnp.float32),
-        in_specs=[VMEM] * 4,
-        out_specs=VMEM,
-        scratch_shapes=[
-            pltpu.VMEM((tiles, bins), jnp.float32),
-            pltpu.VMEM((tiles // together, together, 16, bins), jnp.bfloat16),
+        functools.partial(settle_kernel, scale),
+        out_shape=(
+            jax.ShapeDtypeStruct((owners, share_rows, bins), jnp.bfloat16),
+            jax.ShapeDtypeStruct(split, jnp.float32),
+        ),
+        in_specs=[VMEM] * 5 + [HBM] * 2,
+        out_specs=(VMEM, VMEM),
+        scratch_shapes=[pltpu.VMEM(floor.shape, floor.dtype)] * 2
+        + [
+            pltpu.VMEM((account_count, bins), jnp.float32),
+            pltpu.VMEM((owners, share_rows, bins), jnp.float32),
+            pltpu.VMEM(split, jnp.float32),
+            pltpu.VMEM((share_rows, bins), jnp.bfloat16),
+            pltpu.VMEM(split, jnp.float32),
+            pltpu.VMEM(split[1:], jnp.float32),
         ]
-        + [whole] * 4
-        + [gathered] * 3,
-        compiler_params=pltpu.CompilerParams(vmem_limit_bytes=24*2**20), name="losses",
-    )(low, bound, value, ratio)
+        + [dma((owners,))] * 2
+        + [dma((owners // 2,))] * 4
+        + [dma((events,))] * 4
+        + [dma((5,))],
+        compiler_params=pltpu.CompilerParams(
+            collective_id=number, has_side_effects=True, vmem_limit_bytes=LIMIT
+        ),
+        name="settle",
+    )(lows, bounds, values, ratio, spill, *far([floor, roof]))
 
 
 def per_device(
@@ -596,12 +628,11 @@
         vuln_bias[None, :],
         1,
     )
-    total = losses(low, bound, value, ratio, account_count)
-    (parts,) = exchange(
-        [total.reshape(owners, share_rows, bin_count)], [("terrain", False)], 2
+    scale = account_count / (rows * width * owners)
+    *sorted_cells, level = sort(low, bound, value, ratio, level, account_count)
+    net_loss, portfolio = settle(
+        *sorted_cells, deductible[None, :], limit[None, :], scale, 2
     )
-    scale = account_count / (rows * width * owners)
-    net_loss, portfolio = settle(parts, deductible[None, :], limit[None, :], scale, 3)
     portfolio = portfolio.reshape(share_rows, bin_count)
     return (level[None], net_loss.reshape(1, account_count, bin_count), portfolio)
 

time: 67.6 us -> 50.4 us (0.75)
  the two profiles are of different devices: /device:TPU:0 before, /device:TPU:3 now
where the time goes in v5:
time: 50.4 us; the launch traced here: 50.3 us
  Pallas kernels  48.2 us (96%)
  local copies, waits for them, and re-layouts  1.45 us (3%)
  between operations  0.65 us (1%)
    pallas_call x1, Pallas kernels, settle(): pl.pallas_call(functools.partial(settle_kernel, scale), out_shape=(jax.Sh...  29.8 us
    pallas_call x1, Pallas kernels, front(): pl.pallas_call(front_kernel, out_shape=(jax.ShapeDtypeStruct((rows, width...  10.4 us
    pallas_call x1, Pallas kernels, sort(): pl.pallas_call(sort_kernel, out_shape=(gathered, gathered, gathered, jax....  8.02 us
    unnamed x2, local copies, waits for them, and re-layouts  1.45 us

profile of v5, /device:TPU:3, one launch (start us, length us, event | category | flops | bytes accessed | tf_op | source)
XLA Modules:
  0.0 50.3 jit_solution(3190779375576878024)
XLA Ops:
  0.6 10.4 %front.1 = (f32[32,1024]{1,0:T(8,128)S(1)}, bf16[256,256]{1,0:T(8,128)(2,1)S(1)}, bf16[256,128]{1,0:T(8,128)(2,1)S(1)}, bf16[256,128]{1,0:T(8,128)(2,1)S(1)}, bf16[256,128]{1,0:T(8,128)(2,1)S(1)}) custom-call(f32[32,1024]{1,0:T(8,128)} %bitcast.11, f32[32,1024]{1,0:T(8,128)} %bed_far.1, s32[32,1024]{1,0:T(8,128)} %bitcast.12, s32[384,128]{1,0:T(8,128)} %account_far.1, ...), custom_call_target="tpu_custom_call" | custom-call | tf_op jit(solution)/shard_map/front/pallas_call | solution.py:209
  11.0 8.0 %sort.1 = (f32[8,64,128]{2,1,0:T(8,128)S(1)}, f32[8,64,128]{2,1,0:T(8,128)S(1)}, f32[8,64,128]{2,1,0:T(8,128)S(1)}, bf16[64,4,16,256]{3,2,1,0:T(8,128)(2,1)S(1)}...) custom-call(bf16[256,128]{1,0:T(8,128)(2,1)S(1)} %get-tuple-element.16.low_in, ...), custom_call_target="tpu_custom_call" | custom-call | tf_op jit(solution)/shard_map/sort/pallas_call | solution.py:377
  19.0 29.8 %settle.1 = (bf16[8,128,256]{2,1,0:T(8,128)(2,1)S(1)}, f32[4,32,256]{2,1,0:T(8,128)S(1)}) custom-call(f32[8,64,128]{2,1,0:T(8,128)S(1)} %get-tuple-element.22.lows, f32[8,64,128]{2,1,0:T(8,128)S(1)} %get-tuple-element.23.bounds, f32[8,64,128]{2,1,0:T(8,128)S(1)} %get-tuple-element.24.values, bf16[64,4,16,256]{3,2,1,0:T(8,128)(2,1)S(1)} %get-tuple-element.25.ratio, ...), custom_call_target="tpu_custom_call" | custom-call | tf_op jit(solution)/shard_map/settle/pallas_call | solution.py:575
  48.8 0.8 %copy.16 = bf16[1,1024,256]{2,1,0:T(8,128)(2,1)} copy(bf16[1,1024,256]{2,1,0:T(8,128)(2,1)S(1)} %bitcast.9) | data formatting | bytes 1048576
  49.6 0.7 %copy.17 = f32[128,256]{1,0:T(8,128)} copy(f32[128,256]{1,0:T(8,128)S(1)} %bitcast.10) | data formatting | bytes 262144

commit v6 on v5

--- a/solution.py
+++ b/solution.py
@@ -9,6 +9,7 @@
 
 SUBSTEPS = 8
 CHUNK = 8
+LAG = 2
 LIMIT = 24 * 2**20
 GROUPS = 8
 SPAN = 32
@@ -243,7 +244,7 @@
 
 
 def sort_kernel(
-    low_in, bin_in, value_in, ratio_in, level_in,
+    owners, low_in, bin_in, value_in, ratio_in, level_in,
     lows, bounds, values, ratio, total, level_out,
     ratio_all, low_all, bound_all, value_all, places,
 ):
@@ -263,8 +264,11 @@
     bound = bin_in[...].astype(jnp.float32)
     high = jnp.where(low < 0, 256.0, 0.0) + jnp.where(bound < 0, 512.0, 0.0)
     low = jnp.where(low < 0, low + 256.0, low) + high
-    group = low.astype(jnp.int32) // group_size
-    low_all[...] = low - (group * group_size).astype(jnp.float32)
+    account = low.astype(jnp.int32)
+    share = accounts // owners
+    rows = share // groups
+    group = account % share // rows
+    low_all[...] = (account // share * rows + account % rows).astype(jnp.float32)
     bound_all[...] = jnp.where(bound < 0, bound + 256.0, bound)
     ratio_all[...] = ratio_in[...].astype(jnp.float32)
     value_all[...] = value_in[...].astype(jnp.float32)
@@ -375,7 +379,7 @@
     gathered = jax.ShapeDtypeStruct((GROUPS, bundles, cells), jnp.float32)
     whole = pltpu.VMEM((tiles, cells), jnp.float32)
     return pl.pallas_call(
-        sort_kernel,
+        functools.partial(sort_kernel, lax.axis_size("terrain")),
         out_shape=(
             gathered,
             gathered,
@@ -395,23 +399,20 @@
 def settle_kernel(
     scale, lows, bounds, values, ratio, spill, floor_far, roof_far,
     net_loss, portfolio,
-    floor, roof, total, parts, made, made_low, arrived, summed,
-    sent_part, got_part, sent_low, got_low, sent_more, got_more,
-    sent_net, got_net, sent_sum, got_sum, local,
+    floor, roof, least, most, total, parts, made, made_low, arrived,
+    sent_part, got_part, sent_low, got_low, sent_net, got_net, local,
 ):
-    accounts, bins = total.shape
-    owners, share_rows, _ = parts.shape
-    groups, bundles, cells = lows.shape
-    group_size = accounts // groups
+    groups, owners, share_rows, bins = total.shape
+    _, bundles, cells = lows.shape
+    group_size = owners * share_rows
     capacity = 2 * cells // groups
     together = cells // capacity
-    members = owners // groups
     zero = jnp.zeros((), jnp.bfloat16)
     events = lax.axis_size("event")
     me, group = lax.axis_index("terrain"), lax.axis_index("event")
     terms = [
-        pltpu.make_async_copy(floor_far, floor, local.at[3]),
-        pltpu.make_async_copy(roof_far, roof, local.at[4]),
+        pltpu.make_async_copy(floor_far, floor, local.at[0]),
+        pltpu.make_async_copy(roof_far, roof, local.at[1]),
     ]
     for copy in terms:
         copy.start()
@@ -421,35 +422,82 @@
             pl.semaphore_signal(
                 barrier, inc=1, device_id={axis: lax.rem(mine + hop, size)}, device_id_type=MESH
             )
+    for copy in terms:
+        copy.wait()
+    picked = (groups * share_rows, floor.shape[1])
+    account = lax.broadcasted_iota(jnp.int32, picked, 1)
+    mine = account == lax.broadcasted_iota(jnp.int32, picked, 0) + me * picked[0]
+    for near, wide in ((floor, least), (roof, most)):
+        column = jnp.sum(jnp.where(mine, near[...], 0.0), axis=1, keepdims=True)
+        column = jnp.broadcast_to(column, (picked[0], bins))
+        for h in range(groups):
+            wide[h] = column[h * share_rows : (h + 1) * share_rows]
     pl.semaphore_wait(barrier, owners + events - 2)
 
-    def give(owner):
-        hop = lax.rem(owner - me + owners, owners)
+    def part_copy(h, hop):
+        owner = lax.rem(me + hop, owners)
         return pltpu.make_async_remote_copy(
-            src_ref=total.at[pl.ds(pl.multiple_of(owner * share_rows, share_rows), share_rows)],
-            dst_ref=parts.at[me],
-            send_sem=sent_part.at[hop],
-            recv_sem=got_part.at[hop],
+            src_ref=total.at[h, owner],
+            dst_ref=parts.at[h, me],
+            send_sem=sent_part.at[h, hop],
+            recv_sem=got_part.at[h, hop],
             device_id={"terrain": owner},
             device_id_type=MESH,
         )
+
+    def low_copy(h, hop):
+        return pltpu.make_async_remote_copy(
+            src_ref=made_low.at[h],
+            dst_ref=net_loss.at[me, h],
+            send_sem=sent_low.at[h, hop],
+            recv_sem=got_low.at[h, hop],
+            device_id={"terrain": lax.rem(me + hop, owners)},
+            device_id_type=MESH,
+        )
+
+    def net_copy(h, hop):
+        return pltpu.make_async_remote_copy(
+            src_ref=made.at[h],
+            dst_ref=arrived.at[group, h],
+            send_sem=sent_net.at[h, hop],
+            recv_sem=got_net.at[h, hop],
+            device_id={"event": lax.rem(group + hop, events)},
+            device_id_type=MESH,
+        )
+
+    def give(h):
+        for hop in range(1, owners):
+            part_copy(h, hop).start()
+
+    def finish(h):
+        whole = total[h, me]
+        for hop in range(1, owners):
+            part_copy(h, hop).wait()
+            whole = whole + parts[h, lax.rem(me + owners - hop, owners)]
+        net = jnp.minimum(jnp.maximum(whole * scale - least[h], 0.0), most[h])
+        made[h] = net
+        low = net.astype(made_low.dtype)
+        made_low[h] = low
+        net_loss[me, h] = low
+        for hop in range(1, events):
+            net_copy(h, hop).start()
+        for hop in range(1, owners):
+            low_copy(h, hop).start()
 
     account_id = numbered(group_size, cells, 0)
     bin_id = jnp.concatenate([numbered(16, bins, 1)] * (cells // 16), axis=0)
     span = min(SPAN, bundles)
 
-    def one_group(number, _):
-        h = lax.rem(me // members + 1 + number, groups)
+    def one_group(h, _):
         rows = pl.ds(pl.multiple_of(h * group_size, group_size), group_size)
         turned = [lax.rem(e + groups - h, together) for e in range(together)]
         summed = None
         for c in range(bundles // span):
             if c == bundles // span // 2:
 
-                @pl.when(number > 0)
+                @pl.when(h > 0)
                 def _():
-                    for j in range(members):
-                        give(lax.rem(h + groups - 1, groups) * members + j).start()
+                    give(h - 1)
 
             left, right = [], []
             for block in range(span // CHUNK):
@@ -478,121 +526,60 @@
                 preferred_element_type=jnp.float32,
             )
             summed = part if summed is None else summed + part
-        total[rows, :] = spill[rows, :] + summed
+        summed = summed + spill[rows, :]
+        for t in range(owners):
+            total[h, t] = summed[t * share_rows : (t + 1) * share_rows]
+
+        @pl.when(h >= LAG)
+        def _():
+            finish(h - LAG)
+
         return 0
 
     lax.fori_loop(0, groups, one_group, 0)
-    for j in range(1, members):
-        give(me // members * members + lax.rem(me + j, members)).start()
-
-    own = pl.ds(pl.multiple_of(me * share_rows, share_rows), share_rows)
-    picked = (share_rows, accounts)
-    account = lax.broadcasted_iota(jnp.int32, picked, 1)
-    mine = account == lax.broadcasted_iota(jnp.int32, picked, 0) + me * share_rows
-
-    def of_share(terms):
-        return jnp.sum(jnp.where(mine, terms[...], 0.0), axis=1, keepdims=True)
-
-    for copy in terms:
-        copy.wait()
-    least, most = of_share(floor), of_share(roof)
-    whole = total[own, :]
-    for hop in range(1, owners):
-        give(lax.rem(me + hop, owners)).wait()
-        whole = whole + parts[lax.rem(me + owners - hop, owners)]
-    net = jnp.minimum(jnp.maximum(whole * scale - least, 0.0), most)
-    made[...] = net.reshape(made.shape)
-    made_low[...] = net.astype(made_low.dtype)
-
-    def push(axis, peer, source, target, sent, received):
-        copy = pltpu.make_async_remote_copy(
-            src_ref=source,
-            dst_ref=target,
-            send_sem=sent,
-            recv_sem=received,
-            device_id={axis: peer},
-            device_id_type=MESH,
-        )
-        copy.start()
-        return copy
-
-    nets, sums = [], []
-    for hop in range(1, events):
-        peer = lax.rem(group + hop, events)
-        nets.append(
-            push("event", peer, made.at[peer], arrived.at[group], sent_net.at[hop], got_net.at[hop])
-        )
-    chips = owners // 2
-    partner = me + 1 - 2 * lax.rem(me, 2)
-    lows_sent = []
-    for k in range(1, chips):
-        peer = lax.rem(me + 2 * k, owners)
-        lows_sent.append(
-            push("terrain", peer, made_low, net_loss.at[me], sent_low.at[k], got_low.at[k])
-        )
-    beside = [
-        push("terrain", partner, made_low, net_loss.at[me], sent_more.at[0], got_more.at[0])
-    ]
-    kept = [
-        pltpu.make_async_copy(made_low, net_loss.at[me], local.at[0]),
-        pltpu.make_async_copy(made.at[group], arrived.at[group], local.at[1]),
-    ]
-    for copy in kept:
-        copy.start()
-    kept[1].wait()
-    for copy in nets:
-        copy.wait()
-    whole = arrived[0]
-    for n in range(1, events):
-        whole = whole + arrived[n]
-    summed[...] = whole / events
-    for hop in range(1, events):
-        peer = lax.rem(group + hop, events)
-        sums.append(
-            push("event", peer, summed, portfolio.at[group], sent_sum.at[hop], got_sum.at[hop])
-        )
-    last = pltpu.make_async_copy(summed, portfolio.at[group], local.at[2])
-    last.start()
-    for k in range(1, chips):
-        lows_sent[k - 1].wait()
-        source = lax.rem(me + owners - 2 * k, owners)
-        beside.append(
-            push(
-                "terrain", partner, net_loss.at[source], net_loss.at[source],
-                sent_more.at[k], got_more.at[k],
-            )
-        )
-    for copy in sums + beside + [kept[0], last]:
-        copy.wait()
+    give(groups - 1)
+    for h in range(groups - LAG, groups):
+        finish(h)
+
+    def close(h, _):
+        whole = made[h]
+        for hop in range(1, events):
+            net_copy(h, hop).wait()
+            whole = whole + arrived[lax.rem(group + events - hop, events), h]
+        portfolio[h] = whole / events
+        for hop in range(1, owners):
+            low_copy(h, hop).wait()
+        return 0
+
+    lax.fori_loop(0, groups, close, 0)
 
 
 def settle(lows, bounds, values, ratio, spill, floor, roof, scale, number):
     account_count, bins = spill.shape
+    groups = lows.shape[0]
     owners, events = lax.axis_size("terrain"), lax.axis_size("event")
-    share_rows = account_count // owners
-    split = (events, share_rows // events, bins)
+    share = (groups, account_count // owners // groups, bins)
+    pieces = (groups, owners) + share[1:]
     dma = pltpu.SemaphoreType.DMA
     return pl.pallas_call(
         functools.partial(settle_kernel, scale),
         out_shape=(
-            jax.ShapeDtypeStruct((owners, share_rows, bins), jnp.bfloat16),
-            jax.ShapeDtypeStruct(split, jnp.float32),
+            jax.ShapeDtypeStruct((owners,) + share, jnp.bfloat16),
+            jax.ShapeDtypeStruct(share, jnp.float32),
         ),
         in_specs=[VMEM] * 5 + [HBM] * 2,
         out_specs=(VMEM, VMEM),
         scratch_shapes=[pltpu.VMEM(floor.shape, floor.dtype)] * 2
+        + [pltpu.VMEM(share, jnp.float32)] * 2
+        + [pltpu.VMEM(pieces, jnp.float32)] * 2
         + [
-            pltpu.VMEM((account_count, bins), jnp.float32),
-            pltpu.VMEM((owners, share_rows, bins), jnp.float32),
-            pltpu.VMEM(split, jnp.float32),
-            pltpu.VMEM((share_rows, bins), jnp.bfloat16),
-            pltpu.VMEM(split, jnp.float32),
-            pltpu.VMEM(split[1:], jnp.float32),
+            pltpu.VMEM(share, jnp.float32),
+            pltpu.VMEM(share, jnp.bfloat16),
+            pltpu.VMEM((events,) + share, jnp.float32),
         ]
-        + [dma((owners,))] * 2
-        + [dma((owners // 2,))] * 4
-        + [dma((events,))] * 4
-        + [dma((5,))],
+        + [dma((groups, owners))] * 4
+        + [dma((groups, events))] * 2
+        + [dma((2,))],
         compiler_params=pltpu.CompilerParams(
             collective_id=number, has_side_effects=True, vmem_limit_bytes=LIMIT
         ),

time: 50.4 us -> 53.8 us (1.067)
  the two profiles are of different devices: /device:TPU:3 before, /device:TPU:0 now
where the time goes in v6:
time: 53.8 us; the launch traced here: 53.7 us
  Pallas kernels  51.6 us (96%)
  local copies, waits for them, and re-layouts  1.45 us (3%)
  between operations  0.65 us (1%)
    pallas_call x1, Pallas kernels, settle(): pl.pallas_call(functools.partial(settle_kernel, scale), out_shape=(jax.Sh...  32.2 us
    pallas_call x1, Pallas kernels, front(): pl.pallas_call(front_kernel, out_shape=(jax.ShapeDtypeStruct((rows, width...  11.2 us
    pallas_call x1, Pallas kernels, sort(): pl.pallas_call(functools.partial(sort_kernel, lax.axis_size('terrain')),...  8.15 us
    unnamed x2, local copies, waits for them, and re-layouts  1.45 us

profile of v6, /device:TPU:0, one launch (start us, length us, event | category | flops | bytes accessed | tf_op | source)
XLA Modules:
  0.0 53.7 jit_solution(9183754459903416695)
XLA Ops:
  0.6 11.2 %front.1 = (f32[32,1024]{1,0:T(8,128)S(1)}, bf16[256,256]{1,0:T(8,128)(2,1)S(1)}, bf16[256,128]{1,0:T(8,128)(2,1)S(1)}, bf16[256,128]{1,0:T(8,128)(2,1)S(1)}, bf16[256,128]{1,0:T(8,128)(2,1)S(1)}) custom-call(f32[32,1024]{1,0:T(8,128)} %bitcast.11, f32[32,1024]{1,0:T(8,128)} %bed_far.1, s32[32,1024]{1,0:T(8,128)} %bitcast.12, s32[384,128]{1,0:T(8,128)} %account_far.1, ...), custom_call_target="tpu_custom_call" | custom-call | tf_op jit(solution)/shard_map/front/pallas_call | solution.py:210
  11.9 8.1 %sort.1 = (f32[8,64,128]{2,1,0:T(8,128)S(1)}, f32[8,64,128]{2,1,0:T(8,128)S(1)}, f32[8,64,128]{2,1,0:T(8,128)S(1)}, bf16[64,4,16,256]{3,2,1,0:T(8,128)(2,1)S(1)}...) custom-call(bf16[256,128]{1,0:T(8,128)(2,1)S(1)} %get-tuple-element.16.low_in, ...), custom_call_target="tpu_custom_call" | custom-call | tf_op jit(solution)/shard_map/sort/pallas_call | solution.py:381
  20.0 32.2 %settle.1 = (bf16[8,8,16,256]{3,2,1,0:T(8,128)(2,1)S(1)}, f32[8,16,256]{2,1,0:T(8,128)S(1)}) custom-call(f32[8,64,128]{2,1,0:T(8,128)S(1)} %get-tuple-element.22.lows, f32[8,64,128]{2,1,0:T(8,128)S(1)} %get-tuple-element.23.bounds, f32[8,64,128]{2,1,0:T(8,128)S(1)} %get-tuple-element.24.values, bf16[64,4,16,256]{3,2,1,0:T(8,128)(2,1)S(1)} %get-tuple-element.25.ratio, ...), custom_call_target="tpu_custom_call" | custom-call | tf_op jit(solution)/shard_map/settle/pallas_call | solution.py:564
  52.2 0.8 %copy.16 = bf16[1,1024,256]{2,1,0:T(8,128)(2,1)} copy(bf16[1,1024,256]{2,1,0:T(8,128)(2,1)S(1)} %bitcast.9) | data formatting | bytes 1048576
  53.0 0.7 %copy.17 = f32[128,256]{1,0:T(8,128)} copy(f32[128,256]{1,0:T(8,128)S(1)} %bitcast.10) | data formatting | bytes 262144

commit v7 on v6

--- a/solution.py
+++ b/solution.py
@@ -9,7 +9,6 @@
 
 SUBSTEPS = 8
 CHUNK = 8
-LAG = 2
 LIMIT = 24 * 2**20
 GROUPS = 8
 SPAN = 32
@@ -399,10 +398,12 @@
 def settle_kernel(
     scale, lows, bounds, values, ratio, spill, floor_far, roof_far,
     net_loss, portfolio,
-    floor, roof, least, most, total, parts, made, made_low, arrived,
-    sent_part, got_part, sent_low, got_low, sent_net, got_net, local,
+    floor, roof, least, most, total, pairs, both, parts, made, made_low, arrived,
+    sent_pair, got_pair, sent_part, got_part, sent_low, got_low, sent_more, got_more,
+    sent_net, got_net, local,
 ):
-    groups, owners, share_rows, bins = total.shape
+    groups, _, chips, share_rows, bins = total.shape
+    owners = 2 * chips
     _, bundles, cells = lows.shape
     group_size = owners * share_rows
     capacity = 2 * cells // groups
@@ -434,46 +435,65 @@
             wide[h] = column[h * share_rows : (h + 1) * share_rows]
     pl.semaphore_wait(barrier, owners + events - 2)
 
-    def part_copy(h, hop):
-        owner = lax.rem(me + hop, owners)
+    core, chip = lax.rem(me, 2), me // 2
+    partner = me + 1 - 2 * core
+
+    def remote(source, target, sent, received, axis, peer):
         return pltpu.make_async_remote_copy(
-            src_ref=total.at[h, owner],
-            dst_ref=parts.at[h, me],
-            send_sem=sent_part.at[h, hop],
-            recv_sem=got_part.at[h, hop],
-            device_id={"terrain": owner},
+            src_ref=source,
+            dst_ref=target,
+            send_sem=sent,
+            recv_sem=received,
+            device_id={axis: peer},
             device_id_type=MESH,
         )
 
-    def low_copy(h, hop):
-        return pltpu.make_async_remote_copy(
-            src_ref=made_low.at[h],
-            dst_ref=net_loss.at[me, h],
-            send_sem=sent_low.at[h, hop],
-            recv_sem=got_low.at[h, hop],
-            device_id={"terrain": lax.rem(me + hop, owners)},
-            device_id_type=MESH,
-        )
+    def behind(k):
+        return lax.rem(chip + chips - k, chips)
+
+    def pair_copy(h):
+        return remote(
+            total.at[h, 1 - core], pairs.at[h], sent_pair.at[h], got_pair.at[h], "terrain", partner
+        )
+
+    def part_copy(h, k):
+        to = lax.rem(chip + k, chips)
+        return remote(
+            both.at[h, to], parts.at[h, chip], sent_part.at[h, k], got_part.at[h, k],
+            "terrain", 2 * to + core,
+        )
+
+    def low_copy(h, k):
+        peer = 2 * lax.rem(chip + k, chips) + core if k else partner
+        return remote(
+            made_low.at[h], net_loss.at[me, h], sent_low.at[h, k], got_low.at[h, k],
+            "terrain", peer,
+        )
+
+    def more_copy(h, k):
+        block = net_loss.at[2 * behind(k) + core, h]
+        return remote(block, block, sent_more.at[h, k], got_more.at[h, k], "terrain", partner)
 
     def net_copy(h, hop):
-        return pltpu.make_async_remote_copy(
-            src_ref=made.at[h],
-            dst_ref=arrived.at[group, h],
-            send_sem=sent_net.at[h, hop],
-            recv_sem=got_net.at[h, hop],
-            device_id={"event": lax.rem(group + hop, events)},
-            device_id_type=MESH,
+        return remote(
+            made.at[h], arrived.at[group, h], sent_net.at[h, hop], got_net.at[h, hop],
+            "event", lax.rem(group + hop, events),
         )
 
     def give(h):
-        for hop in range(1, owners):
-            part_copy(h, hop).start()
+        pair_copy(h).start()
+
+    def spread(h):
+        pair_copy(h).wait()
+        both[h] = total[h, core] + pairs[h]
+        for k in range(1, chips):
+            part_copy(h, k).start()
 
     def finish(h):
-        whole = total[h, me]
-        for hop in range(1, owners):
-            part_copy(h, hop).wait()
-            whole = whole + parts[h, lax.rem(me + owners - hop, owners)]
+        whole = both[h, chip]
+        for k in range(1, chips):
+            part_copy(h, k).wait()
+            whole = whole + parts[h, behind(k)]
         net = jnp.minimum(jnp.maximum(whole * scale - least[h], 0.0), most[h])
         made[h] = net
         low = net.astype(made_low.dtype)
@@ -481,24 +501,32 @@
         net_loss[me, h] = low
         for hop in range(1, events):
             net_copy(h, hop).start()
-        for hop in range(1, owners):
-            low_copy(h, hop).start()
+        for k in range(1, chips):
+            low_copy(h, k).start()
+        low_copy(h, 0).start()
+
+    def forward(h):
+        for k in range(1, chips):
+            low_copy(h, k).wait()
+            more_copy(h, k).start()
+
+    stages = ((give, 1), (spread, 2), (finish, 4), (forward, 6))
 
     account_id = numbered(group_size, cells, 0)
     bin_id = jnp.concatenate([numbered(16, bins, 1)] * (cells // 16), axis=0)
     span = min(SPAN, bundles)
 
     def one_group(h, _):
+        for stage, lag in stages[::-1]:
+
+            @pl.when(h >= lag)
+            def _(stage=stage, lag=lag):
+                stage(h - lag)
+
         rows = pl.ds(pl.multiple_of(h * group_size, group_size), group_size)
         turned = [lax.rem(e + groups - h, together) for e in range(together)]
         summed = None
         for c in range(bundles // span):
-            if c == bundles // span // 2:
-
-                @pl.when(h > 0)
-                def _():
-                    give(h - 1)
-
             left, right = [], []
             for block in range(span // CHUNK):
                 first = c * span + block * CHUNK
@@ -528,18 +556,14 @@
             summed = part if summed is None else summed + part
         summed = summed + spill[rows, :]
         for t in range(owners):
-            total[h, t] = summed[t * share_rows : (t + 1) * share_rows]
-
-        @pl.when(h >= LAG)
-        def _():
-            finish(h - LAG)
+            total[h, t % 2, t // 2] = summed[t * share_rows : (t + 1) * share_rows]
 
         return 0
 
     lax.fori_loop(0, groups, one_group, 0)
-    give(groups - 1)
-    for h in range(groups - LAG, groups):
-        finish(h)
+    for stage, lag in stages:
+        for h in range(groups - lag, groups):
+            stage(h)
 
     def close(h, _):
         whole = made[h]
@@ -547,8 +571,9 @@
             net_copy(h, hop).wait()
             whole = whole + arrived[lax.rem(group + events - hop, events), h]
         portfolio[h] = whole / events
-        for hop in range(1, owners):
-            low_copy(h, hop).wait()
+        low_copy(h, 0).wait()
+        for k in range(1, chips):
+            more_copy(h, k).wait()
         return 0
 
     lax.fori_loop(0, groups, close, 0)
@@ -559,7 +584,8 @@
     groups = lows.shape[0]
     owners, events = lax.axis_size("terrain"), lax.axis_size("event")
     share = (groups, account_count // owners // groups, bins)
-    pieces = (groups, owners) + share[1:]
+    chips = owners // 2
+    pieces = (groups, chips) + share[1:]
     dma = pltpu.SemaphoreType.DMA
     return pl.pallas_call(
         functools.partial(settle_kernel, scale),
@@ -571,13 +597,15 @@
         out_specs=(VMEM, VMEM),
         scratch_shapes=[pltpu.VMEM(floor.shape, floor.dtype)] * 2
         + [pltpu.VMEM(share, jnp.float32)] * 2
-        + [pltpu.VMEM(pieces, jnp.float32)] * 2
+        + [pltpu.VMEM((groups, 2, chips) + share[1:], jnp.float32)]
+        + [pltpu.VMEM(pieces, jnp.float32)] * 3
         + [
             pltpu.VMEM(share, jnp.float32),
             pltpu.VMEM(share, jnp.bfloat16),
             pltpu.VMEM((events,) + share, jnp.float32),
         ]
-        + [dma((groups, owners))] * 4
+        + [dma((groups,))] * 2
+        + [dma((groups, chips))] * 6
         + [dma((groups, events))] * 2
         + [dma((2,))],
         compiler_params=pltpu.CompilerParams(

time: 53.8 us -> 49.9 us (0.928)
  Pallas kernels: 51.6 us -> 47.8 us
    pallas_call x1, Pallas kernels: 32.2 us -> 28.5 us  [settle(): pl.pallas_call(functools.partial(settle_kernel, scale), out_shape=(jax.Sh...]
where the time goes in v7:
time: 49.9 us
  Pallas kernels  47.8 us (96%)
  local copies, waits for them, and re-layouts  1.45 us (3%)
  between operations  0.65 us (1%)
    pallas_call x1, Pallas kernels, settle(): pl.pallas_call(functools.partial(settle_kernel, scale), out_shape=(jax.Sh...  28.5 us
    pallas_call x1, Pallas kernels, front(): pl.pallas_call(front_kernel, out_shape=(jax.ShapeDtypeStruct((rows, width...  11.2 us
    pallas_call x1, Pallas kernels, sort(): pl.pallas_call(functools.partial(sort_kernel, lax.axis_size('terrain')),...  8.15 us
    unnamed x2, local copies, waits for them, and re-layouts  1.45 us

profile of v7, /device:TPU:0, one launch (start us, length us, event | category | flops | bytes accessed | tf_op | source)
XLA Modules:
  0.0 49.9 jit_solution(12519923358606803294)
XLA Ops:
  0.6 11.2 %front.1 = (f32[32,1024]{1,0:T(8,128)S(1)}, bf16[256,256]{1,0:T(8,128)(2,1)S(1)}, bf16[256,128]{1,0:T(8,128)(2,1)S(1)}, bf16[256,128]{1,0:T(8,128)(2,1)S(1)}, bf16[256,128]{1,0:T(8,128)(2,1)S(1)}) custom-call(f32[32,1024]{1,0:T(8,128)} %bitcast.11, f32[32,1024]{1,0:T(8,128)} %bed_far.1, s32[32,1024]{1,0:T(8,128)} %bitcast.12, s32[384,128]{1,0:T(8,128)} %account_far.1, ...), custom_call_target="tpu_custom_call" | custom-call | tf_op jit(solution)/shard_map/front/pallas_call | solution.py:209
  11.9 8.1 %sort.1 = (f32[8,64,128]{2,1,0:T(8,128)S(1)}, f32[8,64,128]{2,1,0:T(8,128)S(1)}, f32[8,64,128]{2,1,0:T(8,128)S(1)}, bf16[64,4,16,256]{3,2,1,0:T(8,128)(2,1)S(1)}...) custom-call(bf16[256,128]{1,0:T(8,128)(2,1)S(1)} %get-tuple-element.16.low_in, ...), custom_call_target="tpu_custom_call" | custom-call | tf_op jit(solution)/shard_map/sort/pallas_call | solution.py:380
  20.0 28.5 %settle.1 = (bf16[8,8,16,256]{3,2,1,0:T(8,128)(2,1)S(1)}, f32[8,16,256]{2,1,0:T(8,128)S(1)}) custom-call(f32[8,64,128]{2,1,0:T(8,128)S(1)} %get-tuple-element.22.lows, f32[8,64,128]{2,1,0:T(8,128)S(1)} %get-tuple-element.23.bounds, f32[8,64,128]{2,1,0:T(8,128)S(1)} %get-tuple-element.24.values, bf16[64,4,16,256]{3,2,1,0:T(8,128)(2,1)S(1)} %get-tuple-element.25.ratio, ...), custom_call_target="tpu_custom_call" | custom-call | tf_op jit(solution)/shard_map/settle/pallas_call | solution.py:590
  48.5 0.8 %copy.16 = bf16[1,1024,256]{2,1,0:T(8,128)(2,1)} copy(bf16[1,1024,256]{2,1,0:T(8,128)(2,1)S(1)} %bitcast.9) | data formatting | bytes 1048576
  49.3 0.7 %copy.17 = f32[128,256]{1,0:T(8,128)} copy(f32[128,256]{1,0:T(8,128)S(1)} %bitcast.10) | data formatting | bytes 262144

commit v8 on v7

--- a/solution.py
+++ b/solution.py
@@ -12,7 +12,6 @@
 LIMIT = 24 * 2**20
 GROUPS = 8
 SPAN = 32
-UNROLL = 16
 
 courant = 0.5
 gravity = 1.0
@@ -20,6 +19,13 @@
 VMEM = pl.BlockSpec(memory_space=pltpu.VMEM)
 HBM = pl.BlockSpec(memory_space=pltpu.HBM)
 MESH = pl.DeviceIdType.MESH
+PICK = lax.GatherDimensionNumbers(
+    offset_dims=(),
+    collapsed_slice_dims=(1,),
+    start_index_map=(1,),
+    operand_batching_dims=(0,),
+    start_indices_batching_dims=(0,),
+)
 
 
 def far(arrays):
@@ -234,6 +240,16 @@
     return jnp.concatenate([packed] * (height // 16), axis=0)
 
 
+def over(number, power):
+    assert power & (power - 1) == 0
+    return number >> (power.bit_length() - 1)
+
+
+def rest(number, power):
+    assert power & (power - 1) == 0
+    return number & (power - 1)
+
+
 def numbered(height, width, axis):
     return (
         lax.broadcasted_iota(jnp.int32, (height, width), axis)
@@ -245,7 +261,7 @@
 def sort_kernel(
     owners, low_in, bin_in, value_in, ratio_in, level_in,
     lows, bounds, values, ratio, total, level_out,
-    ratio_all, low_all, bound_all, value_all, places,
+    ratio_all, low_all, bound_all, value_all, places, keys, worths,
 ):
     level_out[...] = level_in[...]
     total[...] = jnp.zeros(total.shape, jnp.float32)
@@ -257,91 +273,89 @@
     together = cells // capacity
     bundles = tiles // together
     zero = jnp.zeros((), jnp.bfloat16)
-    one = jnp.ones((), jnp.bfloat16)
+
+    ratio_all[...] = ratio_in[...].astype(jnp.float32)
+
+    def widen(number, _):
+        for u in range(8):
+            for j in range(together):
+                row = ratio_all[pl.ds((number * 8 + u) * together + j, 1), :]
+                ratio[number * 8 + u, j] = jnp.broadcast_to(row, (16, bins)).astype(jnp.bfloat16)
+        return 0
+
+    lax.fori_loop(0, bundles // 8, widen, 0)
 
     low = low_in[...].astype(jnp.float32)
     bound = bin_in[...].astype(jnp.float32)
+    value = value_in[...].astype(jnp.float32)
     high = jnp.where(low < 0, 256.0, 0.0) + jnp.where(bound < 0, 512.0, 0.0)
-    low = jnp.where(low < 0, low + 256.0, low) + high
-    account = low.astype(jnp.int32)
+    account = (jnp.where(low < 0, low + 256.0, low) + high).astype(jnp.int32)
+    bound = jnp.where(bound < 0, bound + 256.0, bound).astype(jnp.int32)
     share = accounts // owners
     rows = share // groups
-    group = account % share // rows
-    low_all[...] = (account // share * rows + account % rows).astype(jnp.float32)
-    bound_all[...] = jnp.where(bound < 0, bound + 256.0, bound)
-    ratio_all[...] = ratio_in[...].astype(jnp.float32)
-    value_all[...] = value_in[...].astype(jnp.float32)
-    earlier = jnp.where(
-        lax.broadcasted_iota(jnp.int32, (cells, cells), 0)
-        < lax.broadcasted_iota(jnp.int32, (cells, cells), 1),
-        1.0,
-        0.0,
-    ).astype(jnp.bfloat16)
-    turn = lax.broadcasted_iota(jnp.int32, (tiles, cells), 0) % together
-    rank = jnp.zeros((tiles, cells), jnp.float32)
-    for h in range(groups):
-        mine = group == h
-        count = jnp.dot(
-            jnp.where(mine, 1.0, 0.0).astype(jnp.bfloat16),
-            earlier,
-            preferred_element_type=jnp.float32,
-        )
-        rank = jnp.where(mine, count, rank)
-    base = (group // together) * cells + ((group + turn) % together) * capacity
-    fits = rank < capacity
-    places[...] = jnp.where(fits, base.astype(jnp.float32) + rank, -1.0 - group.astype(jnp.float32))
-
-    place_id = numbered(2 * cells, cells, 0)
-    lane = lax.broadcasted_iota(jnp.int32, (8, cells), 1) // capacity
-    field = lax.broadcasted_iota(jnp.int32, (8, cells), 0)
-    unroll = max(1, UNROLL // together)
-
-    def spread(ref, t):
-        return jnp.broadcast_to(ref[pl.ds(t, 1), :], (8, cells))
-
-    def gather(number, _):
-        for u in range(unroll):
-            bundle = number * unroll + u
-            for j in range(together):
-                t = bundle * together + j
-                ratio[bundle, j] = jnp.broadcast_to(
-                    ratio_all[pl.ds(t, 1), :], (16, bins)
-                ).astype(jnp.bfloat16)
-            found = []
-            for j in range(together):
-                t = bundle * together + j
-                here = rowed(places[pl.ds(t, 1), :], 2 * cells) == place_id
-                fields = jnp.where(
-                    field == 0,
-                    spread(low_all, t),
-                    jnp.where(field == 1, spread(bound_all, t), spread(value_all, t)),
-                )
-                found.append(
-                    lax.dot_general(
-                        fields.astype(jnp.bfloat16),
-                        jnp.where(here, one, zero),
-                        (((1,), (1,)), ((), ())),
-                        preferred_element_type=jnp.float32,
-                    )
-                )
-            for q in range(2):
-                parts = [f[:, q * cells : (q + 1) * cells] for f in found]
-                for r in range(together):
-                    mixed = parts[(0 - r) % together]
-                    for e in range(1, together):
-                        mixed = jnp.where(lane == e, parts[(e - r) % together], mixed)
-                    h = q * together + r
-                    lows[h, pl.ds(bundle, 1), :] = mixed[0:1]
-                    bounds[h, pl.ds(bundle, 1), :] = mixed[1:2]
-                    values[h, pl.ds(bundle, 1), :] = mixed[2:3]
-        return 0
-
-    lax.fori_loop(0, bundles // unroll, gather, 0)
-
-    spilled = jnp.max(rank) >= capacity
-
-    @pl.when(spilled)
+    group = over(rest(account, share), rows)
+    low = over(account, share) * rows + rest(account, rows)
+    key = low * 256 + bound
+    first = lax.broadcasted_iota(jnp.int32, (cells, cells), 0)
+    second = lax.broadcasted_iota(jnp.int32, (cells, cells), 1)
+    upto = jnp.where(first <= second, 1.0, 0.0).astype(jnp.bfloat16)
+
+    def counted(h):
+        mine = jnp.where(group == h, 1.0, 0.0).astype(jnp.bfloat16)
+        return jnp.dot(mine, upto, preferred_element_type=jnp.float32)
+
+    lane = lax.broadcasted_iota(jnp.int32, (tiles, cells), 1)
+    turn = rest(lax.broadcasted_iota(jnp.int32, (tiles, cells), 0), together)
+    wanted = rest(lane, capacity)
+    shift = rest(over(lane, capacity) + together - turn, together) * 8
+    largest = jnp.zeros((tiles, cells), jnp.float32)
+
+    def taken(table, place):
+        return lax.gather(
+            table, place[..., None], PICK, (1, 1), mode=lax.GatherScatterMode.PROMISE_IN_BOUNDS
+        )
+
+    for q in range(2):
+        table = jnp.zeros((tiles, cells), jnp.int32)
+        for r in range(together):
+            count = counted(q * together + r)
+            largest = jnp.maximum(largest, count)
+            table = table + lax.shift_left(count.astype(jnp.int32), 8 * r)
+
+        def count_at(place):
+            return lax.shift_right_logical(taken(table, place), shift) & 255
+
+        place = jnp.zeros((tiles, cells), jnp.int32)
+        step = cells // 2
+        while step:
+            place = jnp.where(count_at(place + (step - 1)) <= wanted, place + step, place)
+            step //= 2
+        keys[q] = taken(key, place)
+        worths[q] = jnp.where(count_at(place) > wanted, taken(value, place), 0.0)
+
+    block = over(lax.broadcasted_iota(jnp.int32, (bundles, cells), 1), capacity)
+    for q in range(2):
+        for r in range(together):
+            for source, targets in ((keys, (lows, bounds)), (worths, (values,))):
+                mixed = source[q, pl.ds((0 - r) % together, bundles, stride=together), :]
+                for e in range(1, together):
+                    part = source[q, pl.ds((e - r) % together, bundles, stride=together), :]
+                    mixed = jnp.where(block == e, part, mixed)
+                if len(targets) == 1:
+                    values[q * together + r] = mixed
+                else:
+                    lows[q * together + r] = (mixed >> 8).astype(jnp.float32)
+                    bounds[q * together + r] = (mixed & 255).astype(jnp.float32)
+
+    @pl.when(jnp.max(largest) > capacity)
     def _():
+        late = jnp.zeros((tiles, cells), jnp.float32)
+        for h in range(groups):
+            late = jnp.where((group == h) & (counted(h) > capacity), -1.0 - h, late)
+        places[...] = late
+        low_all[...] = low.astype(jnp.float32)
+        bound_all[...] = bound.astype(jnp.float32)
+        value_all[...] = value
         account_id = numbered(group_size, cells, 0)
         bin_id = jnp.concatenate([numbered(16, bins, 1)] * (cells // 16), axis=0)
         tile_id = lax.broadcasted_iota(jnp.int32, (tiles, cells), 0).astype(jnp.float32)
@@ -349,16 +363,16 @@
         def dense(left_over):
             t = left_over.astype(jnp.int32)
             place = places[pl.ds(t, 1), :]
-            rest = jnp.where(place < 0, value_all[pl.ds(t, 1), :], 0.0)
+            worth = jnp.where(place < 0, value_all[pl.ds(t, 1), :], 0.0)
             hit = rowed(low_all[pl.ds(t, 1), :], group_size) == account_id
-            column = jnp.transpose(spread(bound_all, t)).astype(jnp.bfloat16)[:, 0:1]
+            columns = jnp.transpose(jnp.broadcast_to(bound_all[pl.ds(t, 1), :], (8, cells)))
             right = jnp.where(
-                bin_id >= jnp.broadcast_to(column, (cells, bins)),
+                bin_id >= jnp.broadcast_to(columns.astype(jnp.bfloat16)[:, 0:1], (cells, bins)),
                 rowed(ratio_all[pl.ds(t, 1), :], cells),
                 zero,
             )
             for h in range(groups):
-                part = jnp.where(place == -1.0 - h, rest, 0.0)
+                part = jnp.where(place == -1.0 - h, worth, 0.0)
                 left = jnp.where(hit, rowed(part, group_size), zero)
                 total[pl.ds(h * group_size, group_size), :] += jnp.dot(
                     left, right, preferred_element_type=jnp.float32
@@ -389,7 +403,9 @@
         ),
         in_specs=[VMEM] * 5,
         out_specs=(VMEM,) * 6,
-        scratch_shapes=[pltpu.VMEM((tiles, bins), jnp.float32)] + [whole] * 4,
+        scratch_shapes=[pltpu.VMEM((tiles, bins), jnp.float32)]
+        + [whole] * 4
+        + [pltpu.VMEM((2, tiles, cells), dtype) for dtype in (jnp.int32, jnp.float32)],
         compiler_params=pltpu.CompilerParams(vmem_limit_bytes=LIMIT),
         name="sort",
     )(low, bound, value, ratio, level)

time: 49.9 us -> 44.9 us (0.90)
  Pallas kernels: 47.8 us -> 42.5 us
    pallas_call x1, Pallas kernels: 8.15 us -> 3.24 us  [sort(): pl.pallas_call(functools.partial(sort_kernel, lax.axis_size('terrain')),...]
where the time goes in v8:
time: 44.9 us; the launch traced here: 44.7 us
  Pallas kernels  42.5 us (95%)
  local copies, waits for them, and re-layouts  1.45 us (3%)
  between operations  0.65 us (1%)
    pallas_call x1, Pallas kernels, settle(): pl.pallas_call(functools.partial(settle_kernel, scale), out_shape=(jax.Sh...  28.1 us
    pallas_call x1, Pallas kernels, front(): pl.pallas_call(front_kernel, out_shape=(jax.ShapeDtypeStruct((rows, width...  11.2 us
    pallas_call x1, Pallas kernels, sort(): pl.pallas_call(functools.partial(sort_kernel, lax.axis_size('terrain')),...  3.24 us
    unnamed x2, local copies, waits for them, and re-layouts  1.45 us

profile of v8, /device:TPU:0, one launch (start us, length us, event | category | flops | bytes accessed | tf_op | source)
XLA Modules:
  0.0 44.7 jit_solution(12980335090048075032)
XLA Ops:
  0.6 11.2 %front.1 = (f32[32,1024]{1,0:T(8,128)S(1)}, bf16[256,256]{1,0:T(8,128)(2,1)S(1)}, bf16[256,128]{1,0:T(8,128)(2,1)S(1)}, bf16[256,128]{1,0:T(8,128)(2,1)S(1)}, bf16[256,128]{1,0:T(8,128)(2,1)S(1)}) custom-call(f32[32,1024]{1,0:T(8,128)} %bitcast.11, f32[32,1024]{1,0:T(8,128)} %bed_far.1, s32[32,1024]{1,0:T(8,128)} %bitcast.12, s32[384,128]{1,0:T(8,128)} %account_far.1, ...), custom_call_target="tpu_custom_call" | custom-call | tf_op jit(solution)/shard_map/front/pallas_call | solution.py:215
  11.9 3.2 %sort.1 = (f32[8,64,128]{2,1,0:T(8,128)S(1)}, f32[8,64,128]{2,1,0:T(8,128)S(1)}, f32[8,64,128]{2,1,0:T(8,128)S(1)}, bf16[64,4,16,256]{3,2,1,0:T(8,128)(2,1)S(1)}...) custom-call(bf16[256,128]{1,0:T(8,128)(2,1)S(1)} %get-tuple-element.16.low_in, ...), custom_call_target="tpu_custom_call" | custom-call | tf_op jit(solution)/shard_map/sort/pallas_call | solution.py:394
  15.1 28.1 %settle.1 = (bf16[8,8,16,256]{3,2,1,0:T(8,128)(2,1)S(1)}, f32[8,16,256]{2,1,0:T(8,128)S(1)}) custom-call(f32[8,64,128]{2,1,0:T(8,128)S(1)} %get-tuple-element.22.lows, f32[8,64,128]{2,1,0:T(8,128)S(1)} %get-tuple-element.23.bounds, f32[8,64,128]{2,1,0:T(8,128)S(1)} %get-tuple-element.24.values, bf16[64,4,16,256]{3,2,1,0:T(8,128)(2,1)S(1)} %get-tuple-element.25.ratio, ...), custom_call_target="tpu_custom_call" | custom-call | tf_op jit(solution)/shard_map/settle/pallas_call | solution.py:606
  43.2 0.8 %copy.16 = bf16[1,1024,256]{2,1,0:T(8,128)(2,1)} copy(bf16[1,1024,256]{2,1,0:T(8,128)(2,1)S(1)} %bitcast.9) | data formatting | bytes 1048576
  44.0 0.7 %copy.17 = f32[128,256]{1,0:T(8,128)} copy(f32[128,256]{1,0:T(8,128)S(1)} %bitcast.10) | data formatting | bytes 262144

commit v9 on v8

--- a/solution.py
+++ b/solution.py
@@ -449,8 +449,6 @@
         column = jnp.broadcast_to(column, (picked[0], bins))
         for h in range(groups):
             wide[h] = column[h * share_rows : (h + 1) * share_rows]
-    pl.semaphore_wait(barrier, owners + events - 2)
-
     core, chip = lax.rem(me, 2), me // 2
     partner = me + 1 - 2 * core
 
@@ -533,6 +531,10 @@
     span = min(SPAN, bundles)
 
     def one_group(h, _):
+        @pl.when(h == 1)
+        def _():
+            pl.semaphore_wait(barrier, owners + events - 2)
+
         for stage, lag in stages[::-1]:
 
             @pl.when(h >= lag)
@@ -631,6 +633,30 @@
     )(lows, bounds, values, ratio, spill, *far([floor, roof]))
 
 
+def place_kernel(*refs):
+    sems = refs[-1]
+    count = len(refs) // 2
+    copies = [
+        pltpu.make_async_copy(refs[n], refs[count + n], sems.at[n]) for n in range(count)
+    ]
+    for copy in copies:
+        copy.start()
+    for copy in copies:
+        copy.wait()
+
+
+def place(arrays):
+    return pl.pallas_call(
+        place_kernel,
+        out_shape=[jax.ShapeDtypeStruct(a.shape, a.dtype) for a in arrays],
+        in_specs=[pl.BlockSpec(memory_space=pl.ANY)] * len(arrays),
+        out_specs=[HBM] * len(arrays),
+        scratch_shapes=[pltpu.SemaphoreType.DMA((len(arrays),))],
+        compiler_params=pltpu.CompilerParams(vmem_limit_bytes=2**20),
+        name="place",
+    )(*arrays)
+
+
 def per_device(
     level_start,
     bed_depth,
@@ -664,6 +690,7 @@
     net_loss, portfolio = settle(
         *sorted_cells, deductible[None, :], limit[None, :], scale, 2
     )
+    net_loss, portfolio = place([net_loss, portfolio])
     portfolio = portfolio.reshape(share_rows, bin_count)
     return (level[None], net_loss.reshape(1, account_count, bin_count), portfolio)
 

time: 44.9 us -> 43.6 us (0.971)
  local copies, waits for them, and re-layouts: 1.45 us -> 0 us
    unnamed x2 -> x0, local copies, waits for them, and re-layouts: 1.45 us -> none
    pallas_call x0 -> x1, Pallas kernels: none -> 0.85 us  [place(): pl.pallas_call(place_kernel, out_shape=[jax.ShapeDtypeStruct(a.shape, a.d...]
    pallas_call x1, Pallas kernels: 28.1 us -> 27.4 us  [settle(): pl.pallas_call(functools.partial(settle_kernel, scale), out_shape=(jax.Sh...]
where the time goes in v9:
time: 43.6 us; the launch traced here: 43.3 us
  Pallas kernels  42.7 us (98%)
  between operations  0.65 us (1%)
    pallas_call x1, Pallas kernels, settle(): pl.pallas_call(functools.partial(settle_kernel, scale), out_shape=(jax.Sh...  27.4 us
    pallas_call x1, Pallas kernels, front(): pl.pallas_call(front_kernel, out_shape=(jax.ShapeDtypeStruct((rows, width...  11.2 us
    pallas_call x1, Pallas kernels, sort(): pl.pallas_call(functools.partial(sort_kernel, lax.axis_size('terrain')),...  3.24 us

profile of v9, /device:TPU:0, one launch (start us, length us, event | category | flops | bytes accessed | tf_op | source)
XLA Modules:
  0.0 43.3 jit_solution(8595387397315815642)
XLA Ops:
  0.6 11.2 %front.1 = (f32[32,1024]{1,0:T(8,128)S(1)}, bf16[256,256]{1,0:T(8,128)(2,1)S(1)}, bf16[256,128]{1,0:T(8,128)(2,1)S(1)}, bf16[256,128]{1,0:T(8,128)(2,1)S(1)}, bf16[256,128]{1,0:T(8,128)(2,1)S(1)}) custom-call(f32[32,1024]{1,0:T(8,128)} %bitcast.9, f32[32,1024]{1,0:T(8,128)} %bed_far.1, s32[32,1024]{1,0:T(8,128)} %bitcast.10, s32[384,128]{1,0:T(8,128)} %account_far.1, ...), custom_call_target="tpu_custom_call" | custom-call | tf_op jit(solution)/shard_map/front/pallas_call | solution.py:215
  11.9 3.2 %sort.1 = (f32[8,64,128]{2,1,0:T(8,128)S(1)}, f32[8,64,128]{2,1,0:T(8,128)S(1)}, f32[8,64,128]{2,1,0:T(8,128)S(1)}, bf16[64,4,16,256]{3,2,1,0:T(8,128)(2,1)S(1)}...) custom-call(bf16[256,128]{1,0:T(8,128)(2,1)S(1)} %get-tuple-element.18.low_in, ...), custom_call_target="tpu_custom_call" | custom-call | tf_op jit(solution)/shard_map/sort/pallas_call | solution.py:394
  15.1 27.4 %settle.1 = (bf16[8,8,16,256]{3,2,1,0:T(8,128)(2,1)S(1)}, f32[8,16,256]{2,1,0:T(8,128)S(1)}) custom-call(f32[8,64,128]{2,1,0:T(8,128)S(1)} %get-tuple-element.24.lows, f32[8,64,128]{2,1,0:T(8,128)S(1)} %get-tuple-element.25.bounds, f32[8,64,128]{2,1,0:T(8,128)S(1)} %get-tuple-element.26.values, bf16[64,4,16,256]{3,2,1,0:T(8,128)(2,1)S(1)} %get-tuple-element.27.ratio, ...), custom_call_target="tpu_custom_call" | custom-call | tf_op jit(solution)/shard_map/settle/pallas_call | solution.py:608
  42.5 0.8 %place.1 = (bf16[8,8,16,256]{3,2,1,0:T(8,128)(2,1)}, f32[8,16,256]{2,1,0:T(8,128)}) custom-call(bf16[8,8,16,256]{3,2,1,0:T(8,128)(2,1)S(1)} %get-tuple-element.29.refs_0_, f32[8,16,256]{2,1,0:T(8,128)S(1)} %get-tuple-element.30.refs_1_), custom_call_target="tpu_custom_call" | custom-call | tf_op jit(solution)/shard_map/place/pallas_call | solution.py:649

commit v10 on v9

--- a/solution.py
+++ b/solution.py
@@ -41,7 +41,7 @@
     level_out, ratio_out, low_out, bin_out, value_out,
     level_here, bed_here, wet_here, account, threshold, value, owner_row, weight, bias, loads,
     made, kept, got, level_above, bed_above, wet_above, level_below, bed_below, wet_below,
-    halo_sent, halo_got, cell_sent, cell_got, local,
+    factors, halo_sent, halo_got, cell_sent, cell_got, local,
 ):
     size = lax.axis_size("terrain")
     me = lax.axis_index("terrain")
@@ -130,20 +130,43 @@
     slot = lax.broadcasted_iota(jnp.int32, (tiles, size * room), 1).astype(jnp.float32)
     chosen = jnp.where(slot == owner_column * room + rank, 1.0, 0.0).astype(jnp.bfloat16)
 
-    for copy in reads[4:] + edges:
+    for copy in reads[4:]:
         copy.wait()
+    assert courant * gravity == 0.5
+    quarter = 0.25
+    tall = rows + 2 * SUBSTEPS
     first_row = me * rows - SUBSTEPS
     total_rows = rows * size
-    level = jnp.concatenate([level_above[...], level_here[...], level_below[...]], axis=0)
-    bed = jnp.concatenate([bed_above[...], bed_here[...], bed_below[...]], axis=0)
-    wet = jnp.concatenate([wet_above[...], wet_here[...], wet_below[...]], axis=0)
-    shape = level.shape
-    tall = shape[0]
-    row_id = first_row + lax.broadcasted_iota(jnp.int32, shape, 0)
-    column = lax.broadcasted_iota(jnp.int32, shape, 1)
-    inside = ((row_id >= 0) & (row_id < total_rows)).astype(jnp.float32)
-    not_first = (column > 0).astype(jnp.float32)
-    not_last = (column < width - 1).astype(jnp.float32)
+
+    def inner(first, count):
+        row = first_row + first + lax.broadcasted_iota(jnp.int32, (count, tile), 0)
+        return jnp.where((row >= 0) & (row < total_rows), quarter, 0.0)
+
+    def mark(bits, first):
+        for j in range(blocks):
+            span = slice(j * tile, (j + 1) * tile)
+            here = bits[:, span]
+            weight_here = inner(first, bits.shape[0])
+            for step in range(SUBSTEPS):
+                factor = jnp.where((here & (1 << step)) != 0, weight_here, 0.0)
+                factors[step, j, first : first + bits.shape[0], :] = factor
+
+    mark(wet_here, SUBSTEPS)
+    for copy in edges:
+        copy.wait()
+    mark(wet_above, 0)
+    mark(wet_below, SUBSTEPS + rows)
+    lane = lax.broadcasted_iota(jnp.int32, (tall, tile), 1)
+    at_first, at_last = lane == 0, lane == tile - 1
+    inside = inner(0, tall)
+
+    def stacked(above, here, below):
+        whole = jnp.concatenate([above[...], here[...], below[...]], axis=0)
+        return [whole[:, j * tile : (j + 1) * tile] for j in range(blocks)]
+
+    level = stacked(level_above, level_here, level_below)
+    bed = stacked(bed_above, bed_here, bed_below)
+    level = [jnp.where(inside > 0, field, 0.0) for field in level]
 
     def down(field):
         return pltpu.roll(field, tall - 1, 0)
@@ -151,45 +174,55 @@
     def up(field):
         return pltpu.roll(field, 1, 0)
 
-    def right(field):
-        return pltpu.roll(field, width - 1, 1) * not_last
-
-    def left(field):
-        return pltpu.roll(field, 1, 1) * not_first
-
-    quarter = 0.25
-    assert courant * gravity == 0.5
-    level = level * inside
-    row_speed = jnp.zeros(shape, jnp.float32)
-    col_speed = jnp.zeros(shape, jnp.float32)
+    def right(fields):
+        turned = [pltpu.roll(field, tile - 1, 1) for field in fields] + [0.0]
+        return [jnp.where(at_last, turned[j + 1], turned[j]) for j in range(blocks)]
+
+    def left(fields):
+        turned = [0.0] + [pltpu.roll(field, 1, 1) for field in fields]
+        return [jnp.where(at_first, turned[j], turned[j + 1]) for j in range(blocks)]
+
+    def each(function, *fields):
+        return [function(*of_block) for of_block in zip(*fields)]
+
+    def plus(one, other):
+        return each(lambda a, b: a + b, one, other)
+
+    def minus(one, other):
+        return each(lambda a, b: a - b, one, other)
+
     for step in range(SUBSTEPS):
-        wet_factor = ((wet >> step) & 1).astype(jnp.float32) * (inside * quarter)
+        factor = [factors[step, j] for j in range(blocks)]
         if step:
-            row_flow, col_flow = bed * row_speed, bed * col_speed
-            new_level = (
-                down(level - row_flow) + up(level + row_flow)
-                + (right(level - col_flow) + left(level + col_flow))
-            )
-            new_row = (
-                down(row_speed - level) + up(row_speed + level)
-                + (right(row_speed) + left(row_speed))
-            )
-            new_col = (
-                down(col_speed) + up(col_speed)
-                + (right(col_speed - level) + left(col_speed + level))
-            )
-            row_speed, col_speed = new_row * wet_factor, new_col * wet_factor
+            row_flow = each(lambda a, b: a * b, bed, row_speed)
+            col_flow = each(lambda a, b: a * b, bed, col_speed)
+            new_level = each(
+                lambda d, u, r, l: (down(d) + up(u) + (r + l)) * inside,
+                minus(level, row_flow), plus(level, row_flow),
+                right(minus(level, col_flow)), left(plus(level, col_flow)),
+            )
+            new_row = each(
+                lambda d, u, r, l, f: (down(d) + up(u) + (r + l)) * f,
+                minus(row_speed, level), plus(row_speed, level),
+                right(row_speed), left(row_speed), factor,
+            )
+            col_speed = each(
+                lambda c, r, l, f: (down(c) + up(c) + (r + l)) * f,
+                col_speed, right(minus(col_speed, level)), left(plus(col_speed, level)), factor,
+            )
+            row_speed = new_row
         else:
-            ld, lu, lr, ll = down(level), up(level), right(level), left(level)
-            new_level = ld + lu + (lr + ll)
-            row_speed = (lu - ld) * wet_factor
-            col_speed = (ll - lr) * wet_factor
-        level = new_level * (inside * quarter)
-    level = level[SUBSTEPS : SUBSTEPS + rows]
-    level_out[...] = level
-    pieces = jnp.concatenate(
-        [level[:, j * tile : (j + 1) * tile] for j in range(blocks)], axis=0
-    ).astype(jnp.bfloat16)
+            beside, before = right(level), left(level)
+            new_level = each(
+                lambda c, r, l: (down(c) + up(c) + (r + l)) * inside, level, beside, before
+            )
+            row_speed = each(lambda c, f: (up(c) - down(c)) * f, level, factor)
+            col_speed = each(lambda r, l, f: (l - r) * f, beside, before, factor)
+        level = new_level
+    level = [field[SUBSTEPS : SUBSTEPS + rows] for field in level]
+    for j in range(blocks):
+        level_out[:, j * tile : (j + 1) * tile] = level[j]
+    pieces = jnp.concatenate(level, axis=0).astype(jnp.bfloat16)
     ratio_out[...] = jax.nn.sigmoid(
         jnp.dot(pieces, weight[...], preferred_element_type=jnp.float32) + bias[...]
     ).astype(jnp.bfloat16)
@@ -225,6 +258,7 @@
         + [dma((9,))]
         + [pltpu.VMEM(packed, jnp.bfloat16)] * 3
         + edges * 2
+        + [pltpu.VMEM((SUBSTEPS, width // cells, rows + 2 * SUBSTEPS, cells), jnp.float32)]
         + [dma((6,))] * 2
         + [dma((size,))] * 2
         + [dma((2,))],

time: 43.6 us -> 43.3 us (level)
  no operation moved by 1% of the time
where the time goes in v10:
time: 43.3 us; the launch traced here: 43.1 us
  Pallas kernels  42.5 us (98%)
  between operations  0.65 us (2%)
    pallas_call x1, Pallas kernels, settle(): pl.pallas_call(functools.partial(settle_kernel, scale), out_shape=(jax.Sh...  27.1 us
    pallas_call x1, Pallas kernels, front(): pl.pallas_call(front_kernel, out_shape=(jax.ShapeDtypeStruct((rows, width...  11.2 us
    pallas_call x1, Pallas kernels, sort(): pl.pallas_call(functools.partial(sort_kernel, lax.axis_size('terrain')),...  3.24 us

profile of v10, /device:TPU:0, one launch (start us, length us, event | category | flops | bytes accessed | tf_op | source)
XLA Modules:
  0.0 43.1 jit_solution(13629335982037470450)
XLA Ops:
  0.6 11.2 %front.1 = (f32[32,1024]{1,0:T(8,128)S(1)}, bf16[256,256]{1,0:T(8,128)(2,1)S(1)}, bf16[256,128]{1,0:T(8,128)(2,1)S(1)}, bf16[256,128]{1,0:T(8,128)(2,1)S(1)}, bf16[256,128]{1,0:T(8,128)(2,1)S(1)}) custom-call(f32[32,1024]{1,0:T(8,128)} %bitcast.9, f32[32,1024]{1,0:T(8,128)} %bed_far.1, s32[32,1024]{1,0:T(8,128)} %bitcast.10, s32[384,128]{1,0:T(8,128)} %account_far.1, ...), custom_call_target="tpu_custom_call" | custom-call | tf_op jit(solution)/shard_map/front/pallas_call | solution.py:248
  11.9 3.2 %sort.1 = (f32[8,64,128]{2,1,0:T(8,128)S(1)}, f32[8,64,128]{2,1,0:T(8,128)S(1)}, f32[8,64,128]{2,1,0:T(8,128)S(1)}, bf16[64,4,16,256]{3,2,1,0:T(8,128)(2,1)S(1)}...) custom-call(bf16[256,128]{1,0:T(8,128)(2,1)S(1)} %get-tuple-element.18.low_in, ...), custom_call_target="tpu_custom_call" | custom-call | tf_op jit(solution)/shard_map/sort/pallas_call | solution.py:428
  15.1 27.1 %settle.1 = (bf16[8,8,16,256]{3,2,1,0:T(8,128)(2,1)S(1)}, f32[8,16,256]{2,1,0:T(8,128)S(1)}) custom-call(f32[8,64,128]{2,1,0:T(8,128)S(1)} %get-tuple-element.24.lows, f32[8,64,128]{2,1,0:T(8,128)S(1)} %get-tuple-element.25.bounds, f32[8,64,128]{2,1,0:T(8,128)S(1)} %get-tuple-element.26.values, bf16[64,4,16,256]{3,2,1,0:T(8,128)(2,1)S(1)} %get-tuple-element.27.ratio, ...), custom_call_target="tpu_custom_call" | custom-call | tf_op jit(solution)/shard_map/settle/pallas_call | solution.py:642
  42.3 0.8 %place.1 = (bf16[8,8,16,256]{3,2,1,0:T(8,128)(2,1)}, f32[8,16,256]{2,1,0:T(8,128)}) custom-call(bf16[8,8,16,256]{3,2,1,0:T(8,128)(2,1)S(1)} %get-tuple-element.29.refs_0_, f32[8,16,256]{2,1,0:T(8,128)S(1)} %get-tuple-element.30.refs_1_), custom_call_target="tpu_custom_call" | custom-call | tf_op jit(solution)/shard_map/place/pallas_call | solution.py:683

commit v11 on v10

--- a/solution.py
+++ b/solution.py
@@ -334,15 +334,11 @@
     second = lax.broadcasted_iota(jnp.int32, (cells, cells), 1)
     upto = jnp.where(first <= second, 1.0, 0.0).astype(jnp.bfloat16)
 
-    def counted(h):
-        mine = jnp.where(group == h, 1.0, 0.0).astype(jnp.bfloat16)
-        return jnp.dot(mine, upto, preferred_element_type=jnp.float32)
-
     lane = lax.broadcasted_iota(jnp.int32, (tiles, cells), 1)
     turn = rest(lax.broadcasted_iota(jnp.int32, (tiles, cells), 0), together)
     wanted = rest(lane, capacity)
     shift = rest(over(lane, capacity) + together - turn, together) * 8
-    largest = jnp.zeros((tiles, cells), jnp.float32)
+    order = jnp.zeros((tiles, cells), jnp.float32)
 
     def taken(table, place):
         return lax.gather(
@@ -352,8 +348,13 @@
     for q in range(2):
         table = jnp.zeros((tiles, cells), jnp.int32)
         for r in range(together):
-            count = counted(q * together + r)
-            largest = jnp.maximum(largest, count)
+            mine = group == q * together + r
+            count = jnp.dot(
+                jnp.where(mine, 1.0, 0.0).astype(jnp.bfloat16),
+                upto,
+                preferred_element_type=jnp.float32,
+            )
+            order = jnp.where(mine, count, order)
             table = table + lax.shift_left(count.astype(jnp.int32), 8 * r)
 
         def count_at(place):
@@ -381,40 +382,40 @@
                     lows[q * together + r] = (mixed >> 8).astype(jnp.float32)
                     bounds[q * together + r] = (mixed & 255).astype(jnp.float32)
 
-    @pl.when(jnp.max(largest) > capacity)
+    @pl.when(jnp.max(order) > capacity)
     def _():
-        late = jnp.zeros((tiles, cells), jnp.float32)
-        for h in range(groups):
-            late = jnp.where((group == h) & (counted(h) > capacity), -1.0 - h, late)
-        places[...] = late
+        tile_id = lax.broadcasted_iota(jnp.int32, (tiles, cells), 0)
+        late = (tile_id * groups + group).astype(jnp.float32)
+        places[...] = jnp.where(order > capacity, late, -1.0)
         low_all[...] = low.astype(jnp.float32)
         bound_all[...] = bound.astype(jnp.float32)
         value_all[...] = value
         account_id = numbered(group_size, cells, 0)
         bin_id = jnp.concatenate([numbered(16, bins, 1)] * (cells // 16), axis=0)
-        tile_id = lax.broadcasted_iota(jnp.int32, (tiles, cells), 0).astype(jnp.float32)
 
         def dense(left_over):
-            t = left_over.astype(jnp.int32)
-            place = places[pl.ds(t, 1), :]
-            worth = jnp.where(place < 0, value_all[pl.ds(t, 1), :], 0.0)
-            hit = rowed(low_all[pl.ds(t, 1), :], group_size) == account_id
+            t = over(left_over.astype(jnp.int32), groups)
+            h = rest(left_over.astype(jnp.int32), groups)
+            worth = jnp.where(
+                places[pl.ds(t, 1), :] == left_over, value_all[pl.ds(t, 1), :], 0.0
+            )
+            left = jnp.where(
+                rowed(low_all[pl.ds(t, 1), :], group_size) == account_id,
+                rowed(worth, group_size),
+                zero,
+            )
             columns = jnp.transpose(jnp.broadcast_to(bound_all[pl.ds(t, 1), :], (8, cells)))
             right = jnp.where(
                 bin_id >= jnp.broadcast_to(columns.astype(jnp.bfloat16)[:, 0:1], (cells, bins)),
                 rowed(ratio_all[pl.ds(t, 1), :], cells),
                 zero,
             )
-            for h in range(groups):
-                part = jnp.where(place == -1.0 - h, worth, 0.0)
-                left = jnp.where(hit, rowed(part, group_size), zero)
-                total[pl.ds(h * group_size, group_size), :] += jnp.dot(
-                    left, right, preferred_element_type=jnp.float32
-                )
-            return jnp.max(jnp.where((places[...] < 0) & (tile_id < left_over), tile_id, -1.0))
+            spot = pl.ds(pl.multiple_of(h * group_size, group_size), group_size)
+            total[spot, :] += jnp.dot(left, right, preferred_element_type=jnp.float32)
+            return jnp.max(jnp.where(places[...] < left_over, places[...], -1.0))
 
         lax.while_loop(
-            lambda t: t >= 0, dense, jnp.max(jnp.where(places[...] < 0, tile_id, -1.0))
+            lambda left_over: left_over >= 0, dense, jnp.max(places[...])
         )
 
 
@@ -569,7 +570,7 @@
         def _():
             pl.semaphore_wait(barrier, owners + events - 2)
 
-        for stage, lag in stages[::-1]:
+        for stage, lag in (stages[1], stages[0], stages[2], stages[3]):
 
             @pl.when(h >= lag)
             def _(stage=stage, lag=lag):

time: 43.3 us -> 43.3 us (level)
  no operation moved by 1% of the time
where the time goes in v11:
time: 43.3 us; the launch traced here: 43.1 us
  Pallas kernels  42.4 us (98%)
  between operations  0.65 us (2%)
    pallas_call x1, Pallas kernels, settle(): pl.pallas_call(functools.partial(settle_kernel, scale), out_shape=(jax.Sh...  27.1 us
    pallas_call x1, Pallas kernels, front(): pl.pallas_call(front_kernel, out_shape=(jax.ShapeDtypeStruct((rows, width...  11.2 us
    pallas_call x1, Pallas kernels, sort(): pl.pallas_call(functools.partial(sort_kernel, lax.axis_size('terrain')),...  3.27 us

profile of v11, /device:TPU:0, one launch (start us, length us, event | category | flops | bytes accessed | tf_op | source)
XLA Modules:
  0.0 43.1 jit_solution(1066166723144417142)
XLA Ops:
  0.6 11.2 %front.1 = (f32[32,1024]{1,0:T(8,128)S(1)}, bf16[256,256]{1,0:T(8,128)(2,1)S(1)}, bf16[256,128]{1,0:T(8,128)(2,1)S(1)}, bf16[256,128]{1,0:T(8,128)(2,1)S(1)}, bf16[256,128]{1,0:T(8,128)(2,1)S(1)}) custom-call(f32[32,1024]{1,0:T(8,128)} %bitcast.9, f32[32,1024]{1,0:T(8,128)} %bed_far.1, s32[32,1024]{1,0:T(8,128)} %bitcast.10, s32[384,128]{1,0:T(8,128)} %account_far.1, ...), custom_call_target="tpu_custom_call" | custom-call | tf_op jit(solution)/shard_map/front/pallas_call | solution.py:248
  11.9 3.3 %sort.1 = (f32[8,64,128]{2,1,0:T(8,128)S(1)}, f32[8,64,128]{2,1,0:T(8,128)S(1)}, f32[8,64,128]{2,1,0:T(8,128)S(1)}, bf16[64,4,16,256]{3,2,1,0:T(8,128)(2,1)S(1)}...) custom-call(bf16[256,128]{1,0:T(8,128)(2,1)S(1)} %get-tuple-element.18.low_in, ...), custom_call_target="tpu_custom_call" | custom-call | tf_op jit(solution)/shard_map/sort/pallas_call | solution.py:429
  15.2 27.1 %settle.1 = (bf16[8,8,16,256]{3,2,1,0:T(8,128)(2,1)S(1)}, f32[8,16,256]{2,1,0:T(8,128)S(1)}) custom-call(f32[8,64,128]{2,1,0:T(8,128)S(1)} %get-tuple-element.24.lows, f32[8,64,128]{2,1,0:T(8,128)S(1)} %get-tuple-element.25.bounds, f32[8,64,128]{2,1,0:T(8,128)S(1)} %get-tuple-element.26.values, bf16[64,4,16,256]{3,2,1,0:T(8,128)(2,1)S(1)} %get-tuple-element.27.ratio, ...), custom_call_target="tpu_custom_call" | custom-call | tf_op jit(solution)/shard_map/settle/pallas_call | solution.py:643
  42.2 0.8 %place.1 = (bf16[8,8,16,256]{3,2,1,0:T(8,128)(2,1)}, f32[8,16,256]{2,1,0:T(8,128)}) custom-call(bf16[8,8,16,256]{3,2,1,0:T(8,128)(2,1)S(1)} %get-tuple-element.29.refs_0_, f32[8,16,256]{2,1,0:T(8,128)S(1)} %get-tuple-element.30.refs_1_), custom_call_target="tpu_custom_call" | custom-call | tf_op jit(solution)/shard_map/place/pallas_call | solution.py:684
